TPU v7x, 256 devices: a whole 4x4x8 slice. The times are simulated.
256 devices in a mesh: date: 16 (over z, core), tile: 16 (over x, y).
Axes of the slice: x: 4, y: 4, z: 8, core: 2. Of those that a mesh axis runs over, the one named last changes fastest.
Arguments:
- imagery: bfloat16 [10, 64, 65536], P(None, 'date', 'tile'), may hold values from -6 to 6
- owner: int32 [65536, 1], replicated, may hold values from 0 to 15; in each aligned block of 4096 rows (0 to 4095, 4096 to 8191, ...) at most 1024 rows name the same one
- parcel_local: int32 [65536], replicated, may hold values from 0 to 15
- lift_weight: bfloat16 [10, 128], replicated, may hold values from -2 to 2
- depth_weight: float32 [2, 5, 128], replicated, may hold values from -2.5 to 2.5
- point_weight: bfloat16 [2, 128, 128], replicated, may hold values from -0.5 to 0.5
- bn_mean: float32 [2, 128], replicated, may hold values from -0.5 to 0.5
- bn_var: float32 [2, 128], replicated, may hold values from 0.25 to 4
- bn_gain: float32 [2, 128], replicated, may hold values from 0.5 to 2
- bn_shift: float32 [2, 128], replicated, may hold values from -1 to 1
Outputs:
- parcel_means: float32 [16, 256, 128], P('date', 'tile')
Inputs may be any that keep to these rules, and one draw needn't show every extreme that they name: `owner`: in each aligned block of 4096 rows (the pixels of one tile), no tile index appears more than 1024 times, and some index appears exactly 1024 times.
All inputs are finite; a program needn't handle non-finite values.
Results may differ from a plain program's by a relative error of at most 0.0008.
Values may be sent and summed in bfloat16 or wider, within the bound.
No kernel may reach another device: no remote copies, remote signals or barrier semaphores. Data moves between devices by JAX's collectives and lax.ppermute only.
A program may use at most 128 MiB of HBM per device.

v0:
```python
import math

import jax
import jax.numpy as jnp
from jax import lax
from jax.sharding import PartitionSpec as P

PARC_DEV = 16


epsilon = 1e-05


def layer_stack(series, weights):
    lift_weight, depth_weight, point_weight, bn_mean, bn_var, bn_gain, bn_shift = weights
    hidden = jnp.einsum(
        "bts,bc->tsc", series, lift_weight, preferred_element_type=jnp.float32
    ).astype(jnp.bfloat16)
    for layer in range(depth_weight.shape[0]):
        length = hidden.shape[0]
        half = depth_weight.shape[1] // 2
        widened = jnp.pad(hidden, ((half, half), (0, 0), (0, 0)))
        spread = jnp.zeros(hidden.shape, jnp.float32)
        for tap in range(depth_weight.shape[1]):
            spread = spread + depth_weight[layer, tap] * widened[tap : tap + length]
        spread = spread.astype(jnp.bfloat16)
        mixed = jnp.einsum(
            "tsc,cd->tsd", spread, point_weight[layer], preferred_element_type=jnp.float32
        )
        factor = bn_gain[layer] / jnp.sqrt(bn_var[layer] + epsilon)
        normed = jax.nn.relu((mixed - bn_mean[layer]) * factor + bn_shift[layer])
        hidden = (0.5 * (normed[0::2] + normed[1::2])).astype(jnp.bfloat16)
    return hidden


def local(
    imagery,
    owner,
    parcel_local,
    lift_weight,
    depth_weight,
    point_weight,
    bn_mean,
    bn_var,
    bn_gain,
    bn_shift,
):
    weights = (lift_weight, depth_weight, point_weight, bn_mean, bn_var, bn_gain, bn_shift)
    tiles = lax.axis_size("tile")
    dates = lax.axis_size("date")
    tile_index = lax.axis_index("tile")
    date_index = lax.axis_index("date")
    bands, date_dev, pix_dev = imagery.shape
    owners = owner[:, 0]
    mine = owners == tile_index
    catalog = jnp.arange(PARC_DEV, dtype=jnp.int32)
    counts = jnp.sum(
        ((parcel_local[:, None] == catalog[None, :]) & mine[:, None]).astype(jnp.int32), axis=0
    )
    capacity = 4 * pix_dev // max(tiles, 8)
    share = capacity // dates
    owner_ids = jnp.arange(tiles, dtype=jnp.int32)
    positions = jnp.arange(pix_dev, dtype=jnp.int32)
    own_owner = lax.dynamic_slice_in_dim(owners, tile_index * pix_dev, pix_dev, 0)
    onehot = (own_owner[:, None] == owner_ids[None, :]).astype(jnp.int32)
    running = jnp.cumsum(onehot, axis=0)
    own_rank = jnp.sum(running * onehot, axis=1) - 1
    own_count = jnp.sum(onehot, axis=0)
    table = (
        jnp.zeros((tiles * capacity,), jnp.int32).at[own_owner * capacity + own_rank].set(positions)
    )
    table = table.reshape(tiles, share, dates).transpose(2, 0, 1).reshape(-1)
    rank_send = (
        jnp.arange(share, dtype=jnp.int32)[None, None, :] * dates
        + jnp.arange(dates, dtype=jnp.int32)[:, None, None]
    )
    valid_send = (rank_send < own_count[None, :, None]).reshape(-1)
    rows = imagery.reshape(bands * date_dev, pix_dev).T
    picked = jnp.take(rows, table, axis=0)
    picked = jnp.where(valid_send[:, None], picked, jnp.zeros_like(picked))
    outgoing = picked.T.reshape(bands, date_dev, table.shape[0])
    arrived = lax.all_to_all(
        lax.all_to_all(outgoing, "date", split_axis=2, concat_axis=1, tiled=True),
        "tile",
        split_axis=2,
        concat_axis=2,
        tiled=True,
    )
    grid = owners.reshape(tiles, pix_dev)
    mine_grid = (grid == tile_index).astype(jnp.int32)
    recv_rank = jnp.cumsum(mine_grid, axis=1) - 1
    target = jnp.where(mine_grid == 1, owner_ids[:, None] * capacity + recv_rank, tiles * capacity)
    recv_table = (
        jnp.full((tiles * capacity + 1,), -1, jnp.int32).at[target.reshape(-1)].set(parcel_local)
    )
    slot_ranks = jnp.arange(share, dtype=jnp.int32) * dates + date_index
    slot_parcel = jnp.take(recv_table[:-1].reshape(tiles, capacity), slot_ranks, axis=1).reshape(-1)
    slots = arrived.shape[2]
    block = math.gcd(slots, 512)
    nblocks = slots // block
    pieces = arrived.reshape(bands, arrived.shape[1], nblocks, block).transpose(2, 0, 1, 3)
    labels = slot_parcel.reshape(nblocks, block)

    def run_block(item):
        piece, label = item
        features = layer_stack(piece, weights)
        member = (label[None, :] == catalog[:, None]).astype(jnp.bfloat16)
        return jnp.einsum("qs,jsc->jqc", member, features, preferred_element_type=jnp.float32)

    partial_value = jnp.sum(lax.map(run_block, (pieces, labels)), axis=0)
    sums = lax.psum_scatter(partial_value, "date", scatter_dimension=0, tiled=True)
    return sums / jnp.maximum(counts, 1).astype(jnp.float32)[None, :, None]


def solution(mesh):
    placed = (P(None, "date", "tile"), P(), P(), P(), P(), P(), P(), P(), P(), P())
    return jax.shard_map(
        local, mesh=mesh, in_specs=placed, out_specs=P("date", "tile", None), check_vma=False
    )
```

profile of v0, /device:TPU:96, one launch (start us, length us, event | category | flops | bytes accessed | tf_op | source)
XLA Modules:
  0.0 666.0 jit_solution(5873517295143704459)
XLA Ops:
  6.5 0.7 constant_dynamic-slice_fusion.1
  7.3 4.6 reduce-window.14
  11.9 0.5 slice_reduce_fusion.1
  12.4 0.2 reduce-window.15
  12.6 0.1 broadcast_add_fusion
  12.7 0.3 convert_reduce_fusion.1
  13.0 0.8 compare_select_fusion.4
  13.7 15.6 %scatter_custom_fusion = s32[16384]{0:T(1024)S(1)} fusion(s32[4096]{0:T(1024)S(1)} %bitcast.142, s32[4096]{0:T(1024)S(1)} %iota.39, s32[]{:T(128)} %copy.70), kind=kCustom, calls=%fused_computation.86 | custom fusion | bytes 65540 | tf_op jit(solution)/shard_map/scatter | solution.py:70
  29.3 0.2 reshape.260
  29.5 0.2 copy.46
  29.7 0.1 reshape.263
  29.8 0.1 reshape.261
  29.9 0.1 broadcast_compare_fusion
  30.0 0.1 lt.84
  30.1 1.1 reshape.262
  31.2 0.1 compare_select_fusion.2
  31.3 0.5 copy.47
  31.8 57.4 %gather_fusion = bf16[16384,40]{1,0:T(8,128)(2,1)} fusion(bf16[4096,40]{1,0:T(8,128)(2,1)S(1)} %bitcast.121, s32[16384]{0:T(1024)S(1)} %broadcast_clamp_fusion), kind=kCustom, calls=%fused_computation | custom fusion | bytes 2686976 | tf_op jit(solution)/shard_map/jit(_take)/gather | solution.py:79
  89.2 13.9 %select_bitcast_fusion = bf16[40,16384]{0,1:T(8,128)(2,1)} fusion(bf16[16384,40]{1,0:T(8,128)(2,1)} %gather_fusion, pred[16384]{0:T(1024)(128)(4,1)S(1)} %compare_and_fusion, pred[16384]{0:T(1024)(128)(4,1)S(1)} %lt.84), kind=kLoop, calls=%fused_computation.60 | loop fusion | flops 1310720 | bytes 2654208 | tf_op jit(solution)/shard_map/jit(_where)/select_n | solution.py:80
  103.1 3.5 copy.49
  106.6 0.5 reshape.264
  107.1 16.3 %copy.50 = bf16[10,4,16384]{0,1,2:T(4,128)(2,1)} copy(bf16[10,4,16384]{2,1,0:T(4,128)(2,1)S(1)} %reshape.264) | data formatting | bytes 2621440 | tf_op jit(solution)/shard_map/reshape | solution.py:81
  123.4 27.2 %reshape.312 = bf16[16,2,20480]{2,1,0:T(2,128)(2,1)} reshape(bf16[16384,4,10]{2,1,0:T(4,128)(2,1)} %bitcast.122) | data formatting | bytes 2621440
  150.6 7.7 %all-to-all-start = ((bf16[16,2,20480]{2,1,0:T(2,128)(2,1)}), bf16[16,2,20480]{2,1,0:T(2,128)(2,1)S(1)}, u32[]{:S(2)}, u32[]{:S(2)}) async-start(bf16[16,2,20480]{2,1,0:T(2,128)(2,1)} %reshape.312), calls=%async_computation | async-start | bytes 2621440 | tf_op jit(solution)/shard_map/all_to_all | solution.py:83
  158.3 0.1 broadcast_bitcast_fusion
  158.4 0.3 copy.60
  158.7 1.4 compare_reduce_fusion
  160.1 4.6 reduce-window.16
  164.7 0.5 slice_reduce_fusion
  165.2 0.2 reduce-window.19
  165.4 0.1 add_add_fusion
  165.5 24.6 %all-to-all-done = bf16[16,2,20480]{2,1,0:T(2,128)(2,1)S(1)} async-done(((bf16[16,2,20480]{2,1,0:T(2,128)(2,1)}), bf16[16,2,20480]{2,1,0:T(2,128)(2,1)S(1)}, u32[]{:S(2)}, u32[]{:S(2)}) %all-to-all-start) | async-done | bytes 1310752 | tf_op jit(solution)/shard_map/all_to_all | solution.py:83
  190.1 40.8 %reshape.313 = bf16[16384,4,10]{2,1,0:T(4,128)(2,1)} reshape(bf16[16,2,20480]{2,1,0:T(2,128)(2,1)S(1)} %all-to-all-done) | data formatting | bytes 2621440
  230.9 23.6 %copy.51 = bf16[10,4,16,1024]{3,1,2,0:T(4,128)(2,1)S(1)} copy(bf16[10,4,16,1024]{0,1,3,2:T(4,128)(2,1)} %bitcast.123) | data formatting | bytes 2621440 | tf_op jit(solution)/shard_map/all_to_all | solution.py:83
  254.5 0.3 all_to_all.19
  254.9 4.8 copy.52
  259.7 6.5 reshape.314
  266.2 7.0 %all-to-all-start.1 = ((bf16[16,2,20480]{2,1,0:T(2,128)(2,1)}), bf16[16,2,20480]{2,1,0:T(2,128)(2,1)S(1)}, u32[]{:S(2)}, u32[]{:S(2)}) async-start(bf16[16,2,20480]{2,1,0:T(2,128)(2,1)} %reshape.314), calls=%async_computation.1 | async-start | bytes 2621440 | tf_op jit(solution)/shard_map/all_to_all | solution.py:82
  273.4 0.6 compare_select_fusion
  274.0 0.1 broadcast_in_dim.81
  274.1 240.0 %scatter_custom_fusion.1 = s32[16385]{0:T(1024)S(1)} fusion(s32[65536]{0:T(1024)S(1)} %bitcast.134, s32[65536]{0:T(1024)} %param.14, s32[]{:T(128)} %constant.109.clone.1), kind=kCustom, calls=%fused_computation.83 | custom fusion | bytes 66052 | tf_op jit(solution)/shard_map/scatter | solution.py:94
  514.2 0.2 copy.54
  514.4 0.6 gather_fusion.1
  515.1 0.1 gather.12
  515.2 3.6 reshape.315
  518.8 7.4 %copy.58 = bf16[10,64,2,512]{3,2,1,0:T(2,128)(2,1)S(1)} copy(bf16[10,64,2,512]{1,0,3,2:T(8,128)(2,1)} %bitcast.125) | data formatting | bytes 2621440 | tf_op jit(solution)/shard_map/reshape | solution.py:101
  526.2 0.8 copy.57
  527.1 77.0 %while.13 = (s32[]{:T(128)}, f32[2,16,16,128]{3,2,1,0:T(8,128)}, f32[2,5,128]{2,1,0:T(8,128)S(1)}, bf16[2,10,64,512]{3,1,2,0:T(8,128)(2,1)S(1)}, bf16[10,128]{1,...) while((s32[]{:T(128)}, f32[2,16,16,128]{3,2,1,0:T(8,128)}, ...), condition=%wide.region_9.10_spmd.clone, body=%wide.region_8.9_spmd.clone.sunk | while | flops 1861231104 | bytes 78875824 | solution.py:110
  527.4 4.7 convolution_convert_fusion.2
  532.1 21.0 %add_maximum_fusion.4 = f32[64,512,128]{2,1,0:T(8,128)} fusion(f32[128]{0:T(128)S(1)} %get-tuple-element.364, f32[128]{0:T(128)S(1)} %get-tuple-element.365, f32[128]{0:T(128)S(1)} %get-tuple-element.366, bf16[64,512,128]{2,1,0:T(8,128)(2,1)} %convolution_convert_fusion.2, f32[128]{0:T(128)S(1)} %get-tuple-element.367, ...), kind=kOutput, calls=%fused_computation.5.clone.1 | convolution fusion | flops 1153433600 | bytes 25202688 | tf_op jit(solution)/shard_map/while/body/eval_jaxpr/tsc,cd->tsd/dot_general | solution.py:27
  553.1 6.4 multiply_convert_fusion.10
  559.6 4.9 add_maximum_fusion.5
  564.5 0.5 fusion.47
  565.0 0.7 copy-done.3
  565.8 4.7 convolution_convert_fusion.2
  570.5 21.0 %add_maximum_fusion.4 = f32[64,512,128]{2,1,0:T(8,128)} fusion(f32[128]{0:T(128)S(1)} %get-tuple-element.364, f32[128]{0:T(128)S(1)} %get-tuple-element.365, f32[128]{0:T(128)S(1)} %get-tuple-element.366, bf16[64,512,128]{2,1,0:T(8,128)(2,1)} %convolution_convert_fusion.2, f32[128]{0:T(128)S(1)} %get-tuple-element.367, ...), kind=kOutput, calls=%fused_computation.5.clone.1 | convolution fusion | flops 1153433600 | bytes 25202688 | tf_op jit(solution)/shard_map/while/body/eval_jaxpr/tsc,cd->tsd/dot_general | solution.py:27
  591.5 6.4 multiply_convert_fusion.10
  597.9 4.9 add_maximum_fusion.5
  602.9 0.5 fusion.47
  603.4 0.7 copy-done.3
  604.1 1.6 reduce_sum.38
  605.7 0.8 convert_reduce_fusion
  606.5 51.3 %reduce-scatter.2.cloned.1.call-done = f32[1,16,128]{2,1,0:T(8,128)} async-done(((f32[16,16,128]{2,1,0:T(8,128)}), f32[1,16,128]{2,1,0:T(8,128)}) %reduce-scatter.2.cloned.1.call-update) | async-done | bytes 8208 | tf_op jit(solution)/shard_map/reduce_scatter | solution.py:111
  657.8 1.4 broadcast_divide_fusion
  (56 shorter events, 0.4 us)
Async XLA Ops:
  123.4 35.2 %copy-start = (s32[65536,1]{0,1:T(1,128)S(1)}, s32[65536,1]{0,1:T(1,128)}, u32[]{:S(2)}) copy-start(s32[65536,1]{0,1:T(1,128)} %param.13) | copy-start | bytes 786436
  150.6 39.5 %all-to-all-start = ((bf16[16,2,20480]{2,1,0:T(2,128)(2,1)}), bf16[16,2,20480]{2,1,0:T(2,128)(2,1)S(1)}, u32[]{:S(2)}, u32[]{:S(2)}) async-start(bf16[16,2,20480]{2,1,0:T(2,128)(2,1)} %reshape.312), calls=%async_computation | async-start | bytes 2621440 | tf_op jit(solution)/shard_map/all_to_all | solution.py:83
  254.5 19.6 %copy-start.10 = (f32[2,5,128]{2,0,1:T(2,128)S(1)}, f32[2,5,128]{2,0,1:T(2,128)}, u32[]{:S(2)}) copy-start(f32[2,5,128]{2,0,1:T(2,128)} %param.16) | copy-start | bytes 15364
  266.2 248.9 %all-to-all-start.1 = ((bf16[16,2,20480]{2,1,0:T(2,128)(2,1)}), bf16[16,2,20480]{2,1,0:T(2,128)(2,1)S(1)}, u32[]{:S(2)}, u32[]{:S(2)}) async-start(bf16[16,2,20480]{2,1,0:T(2,128)(2,1)} %reshape.314), calls=%async_computation.1 | async-start | bytes 2621440 | tf_op jit(solution)/shard_map/all_to_all | solution.py:82
  273.3 253.7 %copy-start.5 = (bf16[10,128]{1,0:T(8,128)(2,1)S(1)}, bf16[10,128]{1,0:T(8,128)(2,1)}, u32[]{:S(2)}) copy-start(bf16[10,128]{1,0:T(8,128)(2,1)} %param.15) | copy-start | bytes 7684
  273.3 253.7 %copy-start.6 = (f32[2,128]{1,0:T(2,128)S(1)}, f32[2,128]{1,0:T(2,128)}, u32[]{:S(2)}) copy-start(f32[2,128]{1,0:T(2,128)} %param.20) | copy-start | bytes 3076
  273.3 253.7 %copy-start.7 = (f32[2,128]{1,0:T(2,128)S(1)}, f32[2,128]{1,0:T(2,128)}, u32[]{:S(2)}) copy-start(f32[2,128]{1,0:T(2,128)} %param.19) | copy-start | bytes 3076
  273.3 253.7 %copy-start.8 = (f32[2,128]{1,0:T(2,128)S(1)}, f32[2,128]{1,0:T(2,128)}, u32[]{:S(2)}) copy-start(f32[2,128]{1,0:T(2,128)} %param.21) | copy-start | bytes 3076
  273.3 253.7 %copy-start.9 = (f32[2,128]{1,0:T(2,128)S(1)}, f32[2,128]{1,0:T(2,128)}, u32[]{:S(2)}) copy-start(f32[2,128]{1,0:T(2,128)} %param.18) | copy-start | bytes 3076
  273.3 253.7 %copy-start.11 = (bf16[2,128,128]{2,1,0:T(8,128)(2,1)S(1)}, bf16[2,128,128]{2,1,0:T(8,128)(2,1)}, u32[]{:S(2)}) copy-start(bf16[2,128,128]{2,1,0:T(8,128)(2,1)} %param.17) | copy-start | bytes 196612
  273.4 384.4 %reduce-scatter.2.cloned.1.call-start = ((), (), s32[]{:S(2)}) async-start(), calls=%async_computation.3 | async-start | bytes 139264 | tf_op jit(solution)/shard_map/reduce_scatter | solution.py:111
  527.1 78.7 %copy-start.1 = (s32[65536]{0:T(1024)S(1)}, s32[65536]{0:T(1024)}, u32[]{:S(2)}) copy-start(s32[65536]{0:T(1024)} %param.14) | copy-start | bytes 786436
  527.1 78.7 %copy-start.4 = (pred[65536]{0:T(1024)(128)(4,1)S(1)}, pred[65536]{0:T(1024)(128)(4,1)}, u32[]{:S(2)}) copy-start(pred[65536]{0:T(1024)(128)(4,1)} %get-tuple-element.276) | copy-start | bytes 196612
  559.6 5.0 copy-start.2
  565.0 0.7 copy-start.3
  597.9 5.0 copy-start.2
  603.4 0.7 copy-start.3
Sparse Core Ops, SparseCore 0:
  605.8 51.8 reduce-scatter.1
where the time goes:
time: 672 us; the launch traced here: 666 us
  local copies, waits for them, and re-layouts  455 us (68%)
  waiting for transfers between devices  75.9 us (11%)
  matrix products  62.3 us (9%)
  other arithmetic  43.7 us (7%)
  starting transfers between devices  14.8 us (2%)
  between operations  13.8 us (2%)
    scatter x1, local copies, waits for them, and re-layouts, local(): jnp.full((tiles * capacity + 1,), -1, jnp.int32).at[target.reshape(-1)]  240 us
    unnamed x28, local copies, waits for them, and re-layouts  79.4 us
    gather x1, local copies, waits for them, and re-layouts, local(): picked = jnp.take(rows, table, axis=0)  57.4 us
    dot_general x4, matrix products, layer_stack(): jnp.einsum('tsc,cd->tsd', spread, point_weight[layer], preferred_element_...  52 us
    reduce_scatter x1, waiting for transfers between devices, local(): lax.psum_scatter(partial_value, 'date', scatter_dimension=0, tiled=True)  51.3 us
    all_to_all x3, local copies, waits for them, and re-layouts, local(): lax.all_to_all(outgoing, 'date', split_axis=2, concat_axis=1, tiled=True)  28.7 us
    all_to_all x1, waiting for transfers between devices, local(): lax.all_to_all(outgoing, 'date', split_axis=2, concat_axis=1, tiled=True)  24.6 us
    reshape x2, local copies, waits for them, and re-layouts, local(): outgoing = picked.T.reshape(bands, date_dev, table.shape[0])  16.8 us
  transfers between devices with their start and end apart: 3, of which 2 were waited for; matrix products, arithmetic and copies ran while one was open for 37% of the time, Pallas kernels for 0%

commit v1 on v0

v1 whole, which is shorter than its diff:
```python
import jax
import jax.numpy as jnp
import numpy as np
from jax import lax
from jax.experimental import pallas as pl
from jax.experimental.pallas import tpu as pltpu
from jax.sharding import PartitionSpec as P

PARC_DEV = 16
EPSILON = 1e-05
SECTION = 48
BLOCK = 1024

SECTIONS = ((-6, 2), (-4, 4), (0, 4), (4, 4), (8, 2))
FIRST = (0, 1, 1, 2, 2, 3)


def column_table(bands, taps):
    table = np.full((12, 4 * SECTION), -1, np.int32)
    for v in range(6):
        for e in range(2):
            out_date = 2 * (v - 2) + e
            for h in range(2):
                base = h * 16 * taps
                for s in range(2):
                    first, held = SECTIONS[FIRST[v] + s]
                    start = h * 2 * SECTION + s * SECTION
                    for b in range(bands):
                        for t in range(held):
                            k = first + t - out_date + taps // 2
                            if 0 <= k < taps:
                                table[2 * v + e, start + b * held + t] = base + k * 16 + b
                ones = 1 if v == 0 else 0
                table[2 * v + e, h * 2 * SECTION + ones * SECTION + 40] = base + bands
    return table


def prep_kernel(where_ref, table_ref, lift_ref, depth_ref, point_ref, mean_ref, var_ref, gain_ref,
                shift_ref, owner_ref, parcel_ref, w0_ref, w1_ref, b1_ref, counts_ref):
    f32, bf16 = jnp.float32, jnp.bfloat16
    taps = depth_ref.shape[1]
    date_index, tile_index = where_ref[0], where_ref[1]
    factor = gain_ref[...] / jnp.sqrt(var_ref[...] + EPSILON)
    shift = 0.5 * (shift_ref[...] - mean_ref[...] * factor)
    factor = 0.5 * factor
    lift = lift_ref[...]
    rows = jnp.concatenate([lift * depth_ref[0, k : k + 1, :] for k in range(taps)], axis=0)
    base = jnp.dot(rows, point_ref[0].astype(f32), precision=lax.Precision.HIGHEST,
                   preferred_element_type=f32) * factor[0:1]
    place = lax.broadcasted_iota(jnp.int32, base.shape, 0)
    base = jnp.where(place == 10, shift[0:1], base)
    high = base.astype(bf16).astype(f32)
    low = base - high
    spare = jnp.zeros((256 - 2 * base.shape[0], base.shape[1]), f32)
    both = jnp.concatenate([high, low, spare], axis=0).T.astype(bf16)
    width = table_ref.shape[1]
    lane_rows = lax.broadcasted_iota(jnp.int32, (256, width), 0)
    for n in range(12):
        pick = jnp.where(lane_rows == table_ref[n : n + 1, :], 1.0, 0.0).astype(bf16)
        w0_ref[n * 128 : (n + 1) * 128, :] = jnp.dot(
            both, pick, preferred_element_type=f32
        ).astype(bf16)
    mix = (point_ref[1].astype(f32) * factor[1:2]).T
    w1_ref[...] = jnp.zeros(w1_ref.shape, bf16)
    for e in range(2):
        for k in range(taps):
            j = k + e
            pooled_date = 2 * date_index - 2 + j
            inside = jnp.logical_and(pooled_date >= 0, pooled_date < 2 * where_ref[2])
            block = mix * depth_ref[1, k : k + 1, :] * jnp.where(inside, 1.0, 0.0)
            block_high = block.astype(bf16)
            w1_ref[e * 128 : (e + 1) * 128, j * 128 : (j + 1) * 128] = block_high
            w1_ref[e * 128 : (e + 1) * 128, 768 + j * 128 : 768 + (j + 1) * 128] = (
                block - block_high.astype(f32)
            ).astype(bf16)
    b1_ref[...] = jnp.broadcast_to(shift[1:2], b1_ref.shape).T
    mine = jnp.where(owner_ref[...] == tile_index, parcel_ref[...], -1)
    for q in range(PARC_DEV):
        hits = jnp.sum(jnp.where(mine == q, 1.0, 0.0), axis=0, keepdims=True)
        counts_ref[q : q + 1, :] = jnp.broadcast_to(
            jnp.sum(hits, axis=1, keepdims=True), (1, 128)
        )


def main_kernel(m2_ref, m1_ref, own_ref, p1_ref, p2_ref, w0_ref, w1_ref, b1_ref, parcel_ref,
                out_ref, stack_ref):
    f32, bf16 = jnp.float32, jnp.bfloat16
    stack_ref[...] = jnp.zeros(stack_ref.shape, bf16)
    for s in (1, 2, 3):
        row = lax.broadcasted_iota(jnp.int32, (16, BLOCK), 0)
        stack_ref[s * SECTION + 32 : s * SECTION + 48, :] = jnp.where(row == 8, 1.0, 0.0).astype(bf16)
    bias = b1_ref[:, 0:1]

    def pooled_pair(values):
        return (jnp.maximum(values[:128], 0.0) + jnp.maximum(values[128:], 0.0)).astype(bf16)

    def stacked(section):
        part = stack_ref[section * SECTION : (section + 2) * SECTION, :]
        return jnp.concatenate([part, part], axis=0)

    def step(i, total):
        columns = pl.ds(pl.multiple_of(i * BLOCK, BLOCK), BLOCK)
        for s, ref in enumerate((m2_ref, m1_ref, own_ref, p1_ref, p2_ref)):
            held = SECTIONS[s][1]
            for b in range(ref.shape[0]):
                start = s * SECTION + b * held
                stack_ref[start : start + held, :] = ref[b, :, columns]
        pooled = []
        for section, lo, hi in ((0, 0, 1), (1, 1, 3), (2, 3, 5), (3, 5, 6)):
            mixed = jnp.dot(w0_ref[lo * 256 : hi * 256, :], stacked(section),
                            preferred_element_type=f32)
            for v in range(hi - lo):
                pooled.append(pooled_pair(mixed[v * 256 : (v + 1) * 256]))
        series = jnp.concatenate(pooled + pooled, axis=0)
        mixed = jnp.dot(w1_ref[...], series, preferred_element_type=f32)
        features = (
            jnp.maximum(mixed[:128] + bias, 0.0) + jnp.maximum(mixed[128:] + bias, 0.0)
        ).astype(bf16)
        ids = lax.broadcasted_iota(jnp.int32, (out_ref.shape[0], BLOCK), 0)
        member = jnp.where(ids == parcel_ref[:, columns], 1.0, 0.0).astype(bf16)
        return total + lax.dot_general(
            member, features, (((1,), (1,)), ((), ())), preferred_element_type=f32
        )

    out_ref[...] = lax.fori_loop(
        0, own_ref.shape[2] // BLOCK, step, jnp.zeros(out_ref.shape, f32)
    )


def local(imagery, owner, parcel_local, lift_weight, depth_weight, point_weight, bn_mean, bn_var,
          bn_gain, bn_shift):
    tiles = lax.axis_size("tile")
    dates = lax.axis_size("date")
    tile_index = lax.axis_index("tile")
    date_index = lax.axis_index("date")
    bands, date_dev, pix_dev = imagery.shape
    channels = lift_weight.shape[1]
    taps = depth_weight.shape[1]

    def shifted(value, by):
        pairs = [(d, d + by) for d in range(dates) if 0 <= d + by < dates]
        return lax.ppermute(value, "date", pairs)

    before = shifted(imagery, 1)
    after = shifted(imagery, -1)
    before_two = shifted(imagery[:, 2:4], 2)
    after_two = shifted(imagery[:, 0:2], -2)

    owners = owner[:, 0]
    parcel = lax.dynamic_slice_in_dim(owners, tile_index * pix_dev, pix_dev) * PARC_DEV
    parcel = parcel + lax.dynamic_slice_in_dim(parcel_local, tile_index * pix_dev, pix_dev)
    table = jnp.asarray(column_table(bands, taps))
    lift = jnp.pad(lift_weight.astype(jnp.float32), ((0, 16 - bands), (0, 0)))
    where = jnp.stack([date_index, tile_index, jnp.int32(dates)]).astype(jnp.int32)
    vmem = pl.BlockSpec(memory_space=pltpu.VMEM)
    w0, w1, b1, counts = pl.pallas_call(
        prep_kernel,
        out_shape=(
            jax.ShapeDtypeStruct((12 * channels, 4 * SECTION), jnp.bfloat16),
            jax.ShapeDtypeStruct((2 * channels, 12 * channels), jnp.bfloat16),
            jax.ShapeDtypeStruct((channels, channels), jnp.float32),
            jax.ShapeDtypeStruct((PARC_DEV, channels), jnp.float32),
        ),
        in_specs=[pl.BlockSpec(memory_space=pltpu.SMEM)] + [vmem] * 10,
        out_specs=(vmem,) * 4,
        name="prep",
    )(where, table, lift, depth_weight, point_weight, bn_mean, bn_var, bn_gain, bn_shift,
      owners.reshape(-1, 128), parcel_local.reshape(-1, 128))
    sums = pl.pallas_call(
        main_kernel,
        out_shape=jax.ShapeDtypeStruct((tiles * PARC_DEV, channels), jnp.float32),
        in_specs=[vmem] * 9,
        out_specs=vmem,
        scratch_shapes=[pltpu.VMEM((5 * SECTION, BLOCK), jnp.bfloat16)],
        name="encode",
    )(before_two, before, imagery, after, after_two, w0, w1, b1, parcel[None, :])
    arrived = lax.all_to_all(sums, "tile", split_axis=0, concat_axis=0, tiled=True)
    total = jnp.sum(arrived.reshape(tiles, PARC_DEV, channels), axis=0)
    return (total / jnp.maximum(counts, 1.0))[None]


def solution(mesh):
    placed = (P(None, "date", "tile"), P(), P(), P(), P(), P(), P(), P(), P(), P())
    return jax.shard_map(
        local, mesh=mesh, in_specs=placed, out_specs=P("date", "tile", None), check_vma=False
    )
```

time: 672 us -> 51.9 us (0.08)
  local copies, waits for them, and re-layouts: 455 us -> 4.36 us
  waiting for transfers between devices: 75.9 us -> 0.01 us
  matrix products: 62.3 us -> 0 us
  other arithmetic: 43.7 us -> 3.84 us
  blocking collectives: 0 us -> 14.9 us
  Pallas kernels: 0 us -> 14.3 us
  between operations: 13.8 us -> 0.12 us
    scatter x2 -> x0, local copies, waits for them, and re-layouts: 256 us -> none  [the longest x1 240 us: local(): jnp.full((tiles * capacity + 1,), -1, jnp.int32).at[target.reshape(-1)]]
    unnamed x28 -> x15, local copies, waits for them, and re-layouts: 79.4 us -> 2.94 us
    dot_general x8 -> x0, matrix products: 62.3 us -> none  [the longest x4 52 us: layer_stack(): jnp.einsum('tsc,cd->tsd', spread, point_weight[layer], preferred_element_...]
    gather x4 -> x0, local copies, waits for them, and re-layouts: 58.1 us -> none  [the longest x1 57.4 us: local(): picked = jnp.take(rows, table, axis=0)]
    reduce_scatter x1 -> x0, waiting for transfers between devices: 51.3 us -> none  [local(): lax.psum_scatter(partial_value, 'date', scatter_dimension=0, tiled=True)]
    all_to_all x3 -> x0, local copies, waits for them, and re-layouts: 28.7 us -> none  [local(): lax.all_to_all(outgoing, 'date', split_axis=2, concat_axis=1, tiled=True)]
    reshape x10 -> x0, local copies, waits for them, and re-layouts: 26.3 us -> none  [the longest x2 16.8 us: local(): outgoing = picked.T.reshape(bands, date_dev, table.shape[0])]
    all_to_all x2 -> x0, waiting for transfers between devices: 24.6 us -> none  [the longest x1 24.6 us: local(): lax.all_to_all(outgoing, 'date', split_axis=2, concat_axis=1, tiled=True)]
  transfers between devices with their start and end apart: 3 -> 4, of which waited for: 2 -> 0; matrix products, arithmetic and copies ran while one was open for 37% -> 10% of each run, Pallas kernels for 0% -> 7%
where the time goes in v1:
time: 51.9 us; the launch traced here: 51.3 us
  blocking collectives  14.9 us (29%)
  Pallas kernels  14.3 us (28%)
  starting transfers between devices  13.7 us (26%)
  local copies, waits for them, and re-layouts  4.36 us (8%)
  other arithmetic  3.84 us (7%)
    all_to_all x1, blocking collectives, local(): lax.all_to_all(sums, 'tile', split_axis=0, concat_axis=0, tiled=True)  14.9 us
    ppermute x4, starting transfers between devices, shifted(): return lax.ppermute(value, 'date', pairs)  13.7 us
    pallas_call x1, Pallas kernels, local(): pl.pallas_call(main_kernel, out_shape=jax.ShapeDtypeStruct((tiles * PARC_...  10.8 us
    pallas_call x1, Pallas kernels, local(): pl.pallas_call(prep_kernel, out_shape=(jax.ShapeDtypeStruct((12 * channel...  3.57 us
    unnamed x15, local copies, waits for them, and re-layouts  2.94 us
    slice x1, local copies, waits for them, and re-layouts, local(): after_two = shifted(imagery[:, 0:2], -2)  1.42 us
    add x1, other arithmetic, local(): parcel + lax.dynamic_slice_in_dim(parcel_local, tile_index * pix_dev, pix...  1.32 us
  transfers between devices with their start and end apart: 4, of which 0 were waited for; matrix products, arithmetic and copies ran while one was open for 10% of the time, Pallas kernels for 7%

profile of v1, /device:TPU:96, one launch (start us, length us, event | category | flops | bytes accessed | tf_op | source)
XLA Modules:
  0.0 51.3 jit_solution(14934988953213568903)
XLA Ops:
  0.0 1.9 %collective-permute-start.1 = (bf16[10,4,4096]{2,1,0:T(4,128)(2,1)}, bf16[10,4,4096]{2,1,0:T(4,128)(2,1)S(1)}, u32[]{:S(2)}, u32[]{:S(2)}) collective-permute-start(bf16[10,4,4096]{2,1,0:T(4,128)(2,1)} %own_ref.1), channel_id=1, source_target_pairs={{0,16},{16,32},{32,48},{48,64},{64,80},{80,96},{96,112},{112,128},... | collective-permute-start | bytes 983048 | tf_op jit(solution)/shard_map/ppermute | solution.py:142
  1.9 3.6 %collective-permute-start.2 = (bf16[10,4,4096]{2,1,0:T(4,128)(2,1)}, bf16[10,4,4096]{2,1,0:T(4,128)(2,1)S(1)}, u32[]{:S(2)}, u32[]{:S(2)}) collective-permute-start(bf16[10,4,4096]{2,1,0:T(4,128)(2,1)} %own_ref.1), channel_id=1, source_target_pairs={{16,0},{32,16},{48,32},{64,48},{80,64},{96,80},{112,96},{128,112},... | collective-permute-start | bytes 983048 | tf_op jit(solution)/shard_map/ppermute | solution.py:142
  5.6 1.4 %fusion = (bf16[10,2,4096]{2,1,0:T(2,128)(2,1)S(1)}, bf16[10,2,4096]{2,1,0:T(2,128)(2,1)S(1)}) fusion(bf16[10,4,4096]{2,1,0:T(4,128)(2,1)} %own_ref.1), kind=kLoop, calls=%fused_computation.5 | loop fusion | bytes 655360 | tf_op jit(solution)/shard_map/slice | solution.py:147
  7.0 2.0 %collective-permute-start.3 = (bf16[10,2,4096]{2,1,0:T(2,128)(2,1)S(1)}, bf16[10,2,4096]{2,1,0:T(2,128)(2,1)S(1)}, u32[]{:S(2)}, u32[]{:S(2)}) collective-permute-start(bf16[10,2,4096]{2,1,0:T(2,128)(2,1)S(1)} %get-tuple-element.13), channel_id=1, source_target_pairs={{32,0},{48,16},{64,32},{80,48},{96,64},{112,80},{128,96},{144,112}... | collective-permute-start | bytes 491528 | tf_op jit(solution)/shard_map/ppermute | solution.py:142
  9.0 6.2 %collective-permute-start = (bf16[10,2,4096]{2,1,0:T(2,128)(2,1)S(1)}, bf16[10,2,4096]{2,1,0:T(2,128)(2,1)S(1)}, u32[]{:S(2)}, u32[]{:S(2)}) collective-permute-start(bf16[10,2,4096]{2,1,0:T(2,128)(2,1)S(1)} %get-tuple-element.14), channel_id=1, source_target_pairs={{0,32},{16,48},{32,64},{48,80},{64,96},{80,112},{96,128},{112,144}... | collective-permute-start | bytes 491528 | tf_op jit(solution)/shard_map/ppermute | solution.py:142
  15.2 0.0 copy-start.6
  15.2 0.7 %copy-done.6 = bf16[10,128]{1,0:T(8,128)(2,1)S(1)} copy-done((bf16[10,128]{1,0:T(8,128)(2,1)S(1)}, bf16[10,128]{1,0:T(8,128)(2,1)}, u32[]{:S(2)}) %copy-start.6) | copy-done | bytes 2584
  15.9 0.0 copy-start.5
  15.9 0.6 %pad_convert_fusion.lift_ref = f32[16,128]{1,0:T(8,128)} fusion(bf16[10,128]{1,0:T(8,128)(2,1)S(1)} %copy-done.6), kind=kLoop, calls=%fused_computation.3 | loop fusion | flops 2048 | bytes 10752 | tf_op jit(solution)/shard_map/jit(_pad)/pad | solution.py:153
  16.5 0.1 copy-done.5
  16.6 0.6 %copy.12.depth_ref = f32[2,5,128]{2,1,0:T(8,128)} copy(f32[2,5,128]{2,0,1:T(2,128)S(1)} %copy-done.5) | data formatting | bytes 10240 | tf_op args[4]
  17.2 0.7 %dynamic-slice_multiply_fusion = s32[4096,1]{0,1:T(1,128)S(1)} fusion(s32[65536,1]{0,1:T(1,128)} %param.12, s32[]{:T(128)S(6)} %select_n.4), kind=kLoop, calls=%fused_computation.1 | loop fusion | flops 4096 | bytes 32772 | tf_op jit(solution)/shard_map/mul | solution.py:150
  17.9 0.6 %pad_add_fusion.where_ref = s32[3]{0:T(128)} fusion(s32[1]{0:T(128)} %constant.9.clone.1, s32[1]{0:T(128)} %bitcast.1, s32[1]{0:T(128)} %bitcast), kind=kLoop, calls=%fused_computation.4 | loop fusion | flops 6 | bytes 24 | tf_op jit(solution)/shard_map/stack | solution.py:154
  18.5 3.6 %prep.1 = (bf16[1536,192]{1,0:T(8,128)(2,1)}, bf16[256,1536]{1,0:T(8,128)(2,1)}, f32[128,128]{1,0:T(8,128)}, f32[16,128]{1,0:T(8,128)}) custom-call(s32[3]{0:T(128)} %pad_add_fusion.where_ref, s32[12,192]{1,0:T(8,128)} %constant.27.clone.table_ref, f32[16,128]{1,0:T(8,128)} %pad_convert_fusion.lift_ref, f32[2,5,128]{2,1,0:T(8,128)} %copy.12.depth_ref, ...), custom_call_target="tpu_custom_call" | custom-call | tf_op jit(solution)/shard_map/prep/pallas_call | solution.py:156
  22.0 1.3 %dynamic-slice_add_fusion = s32[4096]{0:T(1024)} fusion(s32[4096]{0:T(1024)S(1)} %bitcast.13, s32[65536]{0:T(1024)} %param.13, s32[]{:T(128)S(6)} %select_n.4), kind=kLoop, calls=%fused_computation | loop fusion | flops 4096 | bytes 49156 | tf_op jit(solution)/shard_map/add | solution.py:151
  23.4 0.0 collective-permute-done.3.p2_ref
  23.4 0.0 copy-start.2
  23.4 0.0 collective-permute-done.m2_ref
  23.4 0.0 copy-start.3
  23.4 0.0 collective-permute-done.1.m1_ref
  23.4 0.0 copy-start
  23.4 0.0 collective-permute-done.2.p1_ref
  23.4 0.0 copy-start.1
  23.4 0.6 %copy-done.2 = bf16[10,2,4096]{2,1,0:T(2,128)(2,1)} copy-done((bf16[10,2,4096]{2,1,0:T(2,128)(2,1)}, bf16[10,2,4096]{2,1,0:T(2,128)(2,1)S(1)}, u32[]{:S(2)}) %copy-start.2) | copy-done | bytes 163864
  24.0 0.1 copy-done.3
  24.1 0.1 copy-done
  24.2 0.1 copy-done.1
  24.3 10.8 %encode.1 = f32[256,128]{1,0:T(8,128)} custom-call(bf16[10,2,4096]{2,1,0:T(2,128)(2,1)} %copy-done.3, bf16[10,4,4096]{2,1,0:T(4,128)(2,1)} %copy-done, bf16[10,4,4096]{2,1,0:T(4,128)(2,1)} %own_ref.1, bf16[10,4,4096]{2,1,0:T(4,128)(2,1)} %copy-done.1, bf16[10,2,4096]{2,1,0:T(2,128)(2,1)} %copy-done.2, bf16[1536,192]{1,0:T(8,128)(2,1)} %get-tuple-element.9.w0_ref, ...), custom_call_target="tpu_custom_call" | custom-call | tf_op jit(solution)/shard_map/encode/pallas_call | solution.py:169
  35.1 14.9 %all_to_all.9 = f32[16,16,128]{2,1,0:T(8,128)S(1)} all-to-all(f32[16,16,128]{2,1,0:T(8,128)} %bitcast.9), channel_id=1, replica_groups=mesh['date'=16,'tile'=16] {'tile'}, dimensions={0} | all-to-all | bytes 262144 | tf_op jit(solution)/shard_map/all_to_all | solution.py:177
  50.0 0.0 copy-start.4
  50.0 0.7 %copy-done.4 = f32[16,128]{1,0:T(8,128)S(1)} copy-done((f32[16,128]{1,0:T(8,128)S(1)}, f32[16,128]{1,0:T(8,128)}, u32[]{:S(2)}) %copy-start.4) | copy-done | bytes 8216
  50.7 0.6 %divide_bitcast_fusion = f32[1,16,128]{2,1,0:T(8,128)} fusion(f32[16,128]{1,0:T(8,128)S(1)} %reduce_sum.9, f32[16,128]{1,0:T(8,128)S(1)} %copy-done.4), kind=kLoop, calls=%fused_computation.2 | loop fusion | flops 4096 | bytes 24576 | tf_op jit(solution)/shard_map/broadcast_in_dim | solution.py:179
  (1 shorter events, 0.0 us)
Async XLA Ops:
  0.0 23.4 %collective-permute-start.1 = (bf16[10,4,4096]{2,1,0:T(4,128)(2,1)}, bf16[10,4,4096]{2,1,0:T(4,128)(2,1)S(1)}, u32[]{:S(2)}, u32[]{:S(2)}) collective-permute-start(bf16[10,4,4096]{2,1,0:T(4,128)(2,1)} %own_ref.1), channel_id=1, source_target_pairs={{0,16},{16,32},{32,48},{48,64},{64,80},{80,96},{96,112},{112,128},... | collective-permute-start | bytes 983048 | tf_op jit(solution)/shard_map/ppermute | solution.py:142
  1.9 21.5 %collective-permute-start.2 = (bf16[10,4,4096]{2,1,0:T(4,128)(2,1)}, bf16[10,4,4096]{2,1,0:T(4,128)(2,1)S(1)}, u32[]{:S(2)}, u32[]{:S(2)}) collective-permute-start(bf16[10,4,4096]{2,1,0:T(4,128)(2,1)} %own_ref.1), channel_id=1, source_target_pairs={{16,0},{32,16},{48,32},{64,48},{80,64},{96,80},{112,96},{128,112},... | collective-permute-start | bytes 983048 | tf_op jit(solution)/shard_map/ppermute | solution.py:142
  7.0 16.4 %collective-permute-start.3 = (bf16[10,2,4096]{2,1,0:T(2,128)(2,1)S(1)}, bf16[10,2,4096]{2,1,0:T(2,128)(2,1)S(1)}, u32[]{:S(2)}, u32[]{:S(2)}) collective-permute-start(bf16[10,2,4096]{2,1,0:T(2,128)(2,1)S(1)} %get-tuple-element.13), channel_id=1, source_target_pairs={{32,0},{48,16},{64,32},{80,48},{96,64},{112,80},{128,96},{144,112}... | collective-permute-start | bytes 491528 | tf_op jit(solution)/shard_map/ppermute | solution.py:142
  9.0 14.3 %collective-permute-start = (bf16[10,2,4096]{2,1,0:T(2,128)(2,1)S(1)}, bf16[10,2,4096]{2,1,0:T(2,128)(2,1)S(1)}, u32[]{:S(2)}, u32[]{:S(2)}) collective-permute-start(bf16[10,2,4096]{2,1,0:T(2,128)(2,1)S(1)} %get-tuple-element.14), channel_id=1, source_target_pairs={{0,32},{16,48},{32,64},{48,80},{64,96},{80,112},{96,128},{112,144}... | collective-permute-start | bytes 491528 | tf_op jit(solution)/shard_map/ppermute | solution.py:142
  15.2 0.7 %copy-start.6 = (bf16[10,128]{1,0:T(8,128)(2,1)S(1)}, bf16[10,128]{1,0:T(8,128)(2,1)}, u32[]{:S(2)}) copy-start(bf16[10,128]{1,0:T(8,128)(2,1)} %param.14) | copy-start | bytes 7684
  15.9 0.7 %copy-start.5 = (f32[2,5,128]{2,0,1:T(2,128)S(1)}, f32[2,5,128]{2,0,1:T(2,128)}, u32[]{:S(2)}) copy-start(f32[2,5,128]{2,0,1:T(2,128)} %param.15) | copy-start | bytes 15364
  23.4 0.7 %copy-start.2 = (bf16[10,2,4096]{2,1,0:T(2,128)(2,1)}, bf16[10,2,4096]{2,1,0:T(2,128)(2,1)S(1)}, u32[]{:S(2)}) copy-start(bf16[10,2,4096]{2,1,0:T(2,128)(2,1)S(1)} %collective-permute-done.3.p2_ref) | copy-start | bytes 491524
  23.4 0.7 %copy-start.3 = (bf16[10,2,4096]{2,1,0:T(2,128)(2,1)}, bf16[10,2,4096]{2,1,0:T(2,128)(2,1)S(1)}, u32[]{:S(2)}) copy-start(bf16[10,2,4096]{2,1,0:T(2,128)(2,1)S(1)} %collective-permute-done.m2_ref) | copy-start | bytes 491524
  23.4 0.8 %copy-start = (bf16[10,4,4096]{2,1,0:T(4,128)(2,1)}, bf16[10,4,4096]{2,1,0:T(4,128)(2,1)S(1)}, u32[]{:S(2)}) copy-start(bf16[10,4,4096]{2,1,0:T(4,128)(2,1)S(1)} %collective-permute-done.1.m1_ref) | copy-start | bytes 983044
  23.4 0.9 %copy-start.1 = (bf16[10,4,4096]{2,1,0:T(4,128)(2,1)}, bf16[10,4,4096]{2,1,0:T(4,128)(2,1)S(1)}, u32[]{:S(2)}) copy-start(bf16[10,4,4096]{2,1,0:T(4,128)(2,1)S(1)} %collective-permute-done.2.p1_ref) | copy-start | bytes 983044
  50.0 0.7 %copy-start.4 = (f32[16,128]{1,0:T(8,128)S(1)}, f32[16,128]{1,0:T(8,128)}, u32[]{:S(2)}) copy-start(f32[16,128]{1,0:T(8,128)} %get-tuple-element.12) | copy-start | bytes 24580

commit v2 on v1

--- a/solution.py
+++ b/solution.py
@@ -1,3 +1,5 @@
+import functools
+
 import jax
 import jax.numpy as jnp
 import numpy as np
@@ -35,16 +37,18 @@
     return table
 
 
-def prep_kernel(where_ref, table_ref, lift_ref, depth_ref, point_ref, mean_ref, var_ref, gain_ref,
-                shift_ref, owner_ref, parcel_ref, w0_ref, w1_ref, b1_ref, counts_ref):
+def prep_kernel(date_ref, tile_ref, table_ref, lift_ref, depth_ref, point_ref, mean_ref, var_ref,
+                gain_ref, shift_ref, owner_ref, parcel_ref, w0_ref, w1_ref, columns_ref,
+                counts_ref, ids_ref, *, dates):
     f32, bf16 = jnp.float32, jnp.bfloat16
-    taps = depth_ref.shape[1]
-    date_index, tile_index = where_ref[0], where_ref[1]
+    taps = depth_ref.shape[0]
+    date_index, tile_index = date_ref[0], tile_ref[0]
     factor = gain_ref[...] / jnp.sqrt(var_ref[...] + EPSILON)
     shift = 0.5 * (shift_ref[...] - mean_ref[...] * factor)
     factor = 0.5 * factor
-    lift = lift_ref[...]
-    rows = jnp.concatenate([lift * depth_ref[0, k : k + 1, :] for k in range(taps)], axis=0)
+    lift = lift_ref[...].astype(f32)
+    lift = jnp.concatenate([lift, jnp.zeros((16 - lift.shape[0], lift.shape[1]), f32)], axis=0)
+    rows = jnp.concatenate([lift * depth_ref[k, 0:1, :] for k in range(taps)], axis=0)
     base = jnp.dot(rows, point_ref[0].astype(f32), precision=lax.Precision.HIGHEST,
                    preferred_element_type=f32) * factor[0:1]
     place = lax.broadcasted_iota(jnp.int32, base.shape, 0)
@@ -56,24 +60,25 @@
     width = table_ref.shape[1]
     lane_rows = lax.broadcasted_iota(jnp.int32, (256, width), 0)
     for n in range(12):
-        pick = jnp.where(lane_rows == table_ref[n : n + 1, :], 1.0, 0.0).astype(bf16)
+        pooled_date = 2 * date_index - 2 + n // 2
+        inside = jnp.logical_and(pooled_date >= 0, pooled_date < 2 * dates)
+        level = jnp.where(inside, 1.0, 0.0)
+        pick = jnp.where(lane_rows == table_ref[n : n + 1, :], level, 0.0).astype(bf16)
         w0_ref[n * 128 : (n + 1) * 128, :] = jnp.dot(
             both, pick, preferred_element_type=f32
         ).astype(bf16)
     mix = (point_ref[1].astype(f32) * factor[1:2]).T
-    w1_ref[...] = jnp.zeros(w1_ref.shape, bf16)
-    for e in range(2):
-        for k in range(taps):
-            j = k + e
-            pooled_date = 2 * date_index - 2 + j
-            inside = jnp.logical_and(pooled_date >= 0, pooled_date < 2 * where_ref[2])
-            block = mix * depth_ref[1, k : k + 1, :] * jnp.where(inside, 1.0, 0.0)
-            block_high = block.astype(bf16)
-            w1_ref[e * 128 : (e + 1) * 128, j * 128 : (j + 1) * 128] = block_high
-            w1_ref[e * 128 : (e + 1) * 128, 768 + j * 128 : 768 + (j + 1) * 128] = (
-                block - block_high.astype(f32)
-            ).astype(bf16)
-    b1_ref[...] = jnp.broadcast_to(shift[1:2], b1_ref.shape).T
+    mix_high = mix.astype(bf16)
+    w1_ref[:, :128] = mix_high
+    w1_ref[:, 128:] = (mix - mix_high.astype(f32)).astype(bf16)
+    for k in range(taps):
+        columns_ref[k * 128 : (k + 1) * 128, :] = jnp.broadcast_to(
+            depth_ref[k, 1:2, :], (128, 128)
+        ).T
+    columns_ref[taps * 128 : (taps + 1) * 128, :] = jnp.broadcast_to(shift[1:2], (128, 128)).T
+    held = ids_ref.shape[0]
+    own = pl.ds(pl.multiple_of(tile_index * held, held), held)
+    ids_ref[...] = owner_ref[own, :] * PARC_DEV + parcel_ref[own, :]
     mine = jnp.where(owner_ref[...] == tile_index, parcel_ref[...], -1)
     for q in range(PARC_DEV):
         hits = jnp.sum(jnp.where(mine == q, 1.0, 0.0), axis=0, keepdims=True)
@@ -82,14 +87,16 @@
         )
 
 
-def main_kernel(m2_ref, m1_ref, own_ref, p1_ref, p2_ref, w0_ref, w1_ref, b1_ref, parcel_ref,
-                out_ref, stack_ref):
+def main_kernel(m2_ref, m1_ref, own_ref, p1_ref, p2_ref, w0_ref, w1_ref, columns_ref,
+                ids_ref, out_ref, stack_ref, *, taps):
     f32, bf16 = jnp.float32, jnp.bfloat16
     stack_ref[...] = jnp.zeros(stack_ref.shape, bf16)
     for s in (1, 2, 3):
         row = lax.broadcasted_iota(jnp.int32, (16, BLOCK), 0)
         stack_ref[s * SECTION + 32 : s * SECTION + 48, :] = jnp.where(row == 8, 1.0, 0.0).astype(bf16)
-    bias = b1_ref[:, 0:1]
+
+    def column(k):
+        return jnp.concatenate([columns_ref[k * 128 : (k + 1) * 128, :]] * (BLOCK // 128), axis=1)
 
     def pooled_pair(values):
         return (jnp.maximum(values[:128], 0.0) + jnp.maximum(values[128:], 0.0)).astype(bf16)
@@ -111,13 +118,25 @@
                             preferred_element_type=f32)
             for v in range(hi - lo):
                 pooled.append(pooled_pair(mixed[v * 256 : (v + 1) * 256]))
-        series = jnp.concatenate(pooled + pooled, axis=0)
-        mixed = jnp.dot(w1_ref[...], series, preferred_element_type=f32)
-        features = (
-            jnp.maximum(mixed[:128] + bias, 0.0) + jnp.maximum(mixed[128:] + bias, 0.0)
-        ).astype(bf16)
-        ids = lax.broadcasted_iota(jnp.int32, (out_ref.shape[0], BLOCK), 0)
-        member = jnp.where(ids == parcel_ref[:, columns], 1.0, 0.0).astype(bf16)
+        halves = []
+        for e in range(2):
+            spread = column(0) * pooled[e].astype(f32)
+            for k in range(1, taps):
+                spread = spread + column(k) * pooled[e + k].astype(f32)
+            spread = spread.astype(bf16)
+            mixed = jnp.dot(w1_ref[...], jnp.concatenate([spread, spread], axis=0),
+                            preferred_element_type=f32)
+            halves.append(jnp.maximum(mixed + column(taps), 0.0))
+        features = (halves[0] + halves[1]).astype(bf16)
+        rows = lax.broadcasted_iota(jnp.int32, (out_ref.shape[0], 128), 0)
+        held = BLOCK // 128
+        member = jnp.concatenate(
+            [
+                jnp.where(rows == ids_ref[pl.ds(i * held + m, 1), :], 1.0, 0.0).astype(bf16)
+                for m in range(held)
+            ],
+            axis=1,
+        )
         return total + lax.dot_general(
             member, features, (((1,), (1,)), ((), ())), preferred_element_type=f32
         )
@@ -146,34 +165,32 @@
     before_two = shifted(imagery[:, 2:4], 2)
     after_two = shifted(imagery[:, 0:2], -2)
 
-    owners = owner[:, 0]
-    parcel = lax.dynamic_slice_in_dim(owners, tile_index * pix_dev, pix_dev) * PARC_DEV
-    parcel = parcel + lax.dynamic_slice_in_dim(parcel_local, tile_index * pix_dev, pix_dev)
     table = jnp.asarray(column_table(bands, taps))
-    lift = jnp.pad(lift_weight.astype(jnp.float32), ((0, 16 - bands), (0, 0)))
-    where = jnp.stack([date_index, tile_index, jnp.int32(dates)]).astype(jnp.int32)
     vmem = pl.BlockSpec(memory_space=pltpu.VMEM)
-    w0, w1, b1, counts = pl.pallas_call(
-        prep_kernel,
+    smem = pl.BlockSpec(memory_space=pltpu.SMEM)
+    w0, w1, columns, counts, ids = pl.pallas_call(
+        functools.partial(prep_kernel, dates=dates),
         out_shape=(
             jax.ShapeDtypeStruct((12 * channels, 4 * SECTION), jnp.bfloat16),
-            jax.ShapeDtypeStruct((2 * channels, 12 * channels), jnp.bfloat16),
-            jax.ShapeDtypeStruct((channels, channels), jnp.float32),
+            jax.ShapeDtypeStruct((channels, 2 * channels), jnp.bfloat16),
+            jax.ShapeDtypeStruct(((taps + 1) * channels, channels), jnp.float32),
             jax.ShapeDtypeStruct((PARC_DEV, channels), jnp.float32),
+            jax.ShapeDtypeStruct((pix_dev // 128, 128), jnp.int32),
         ),
-        in_specs=[pl.BlockSpec(memory_space=pltpu.SMEM)] + [vmem] * 10,
-        out_specs=(vmem,) * 4,
+        in_specs=[smem] * 2 + [vmem] * 10,
+        out_specs=(vmem,) * 5,
         name="prep",
-    )(where, table, lift, depth_weight, point_weight, bn_mean, bn_var, bn_gain, bn_shift,
-      owners.reshape(-1, 128), parcel_local.reshape(-1, 128))
+    )(date_index.reshape(1), tile_index.reshape(1), table, lift_weight,
+      depth_weight.transpose(1, 0, 2), point_weight, bn_mean, bn_var, bn_gain, bn_shift,
+      owner.reshape(-1, 128), parcel_local.reshape(-1, 128))
     sums = pl.pallas_call(
-        main_kernel,
+        functools.partial(main_kernel, taps=taps),
         out_shape=jax.ShapeDtypeStruct((tiles * PARC_DEV, channels), jnp.float32),
         in_specs=[vmem] * 9,
         out_specs=vmem,
         scratch_shapes=[pltpu.VMEM((5 * SECTION, BLOCK), jnp.bfloat16)],
         name="encode",
-    )(before_two, before, imagery, after, after_two, w0, w1, b1, parcel[None, :])
+    )(before_two, before, imagery, after, after_two, w0, w1, columns, ids)
     arrived = lax.all_to_all(sums, "tile", split_axis=0, concat_axis=0, tiled=True)
     total = jnp.sum(arrived.reshape(tiles, PARC_DEV, channels), axis=0)
     return (total / jnp.maximum(counts, 1.0))[None]

time: 51.9 us -> 46.5 us (0.90)
  the two profiles are of different devices: /device:TPU:96 before, /device:TPU:128 now
where the time goes in v2:
time: 46.5 us; the launch traced here: 46.1 us
  blocking collectives  14.9 us (32%)
  Pallas kernels  12.8 us (28%)
  starting transfers between devices  12.6 us (27%)
  local copies, waits for them, and re-layouts  2.99 us (6%)
  waiting for transfers between devices  2.14 us (5%)
  other arithmetic  0.63 us (1%)
    all_to_all x1, blocking collectives, local(): lax.all_to_all(sums, 'tile', split_axis=0, concat_axis=0, tiled=True)  14.9 us
    ppermute x4, starting transfers between devices, shifted(): return lax.ppermute(value, 'date', pairs)  12.6 us
    pallas_call x1, Pallas kernels, local(): pl.pallas_call(functools.partial(main_kernel, taps=taps), out_shape=jax.S...  9.56 us
    pallas_call x1, Pallas kernels, local(): pl.pallas_call(functools.partial(prep_kernel, dates=dates), out_shape=(ja...  3.24 us
    ppermute x4, waiting for transfers between devices, shifted(): return lax.ppermute(value, 'date', pairs)  2.14 us
    unnamed x10, local copies, waits for them, and re-layouts  1.58 us
    slice x1, local copies, waits for them, and re-layouts, local(): after_two = shifted(imagery[:, 0:2], -2)  1.42 us
  transfers between devices with their start and end apart: 4, of which 1 were waited for; matrix products, arithmetic and copies ran while one was open for 3% of the time, Pallas kernels for 7%

profile of v2, /device:TPU:128, one launch (start us, length us, event | category | flops | bytes accessed | tf_op | source)
XLA Modules:
  0.0 46.1 jit_solution(2554451762198885945)
XLA Ops:
  0.0 1.9 %collective-permute-start.1 = (bf16[10,4,4096]{2,1,0:T(4,128)(2,1)}, bf16[10,4,4096]{2,1,0:T(4,128)(2,1)S(1)}, u32[]{:S(2)}, u32[]{:S(2)}) collective-permute-start(bf16[10,4,4096]{2,1,0:T(4,128)(2,1)} %own_ref.1), channel_id=1, source_target_pairs={{0,16},{16,32},{32,48},{48,64},{64,80},{80,96},{96,112},{112,128},... | collective-permute-start | bytes 983048 | tf_op jit(solution)/shard_map/ppermute | solution.py:161
  1.9 4.9 %collective-permute-start.2 = (bf16[10,4,4096]{2,1,0:T(4,128)(2,1)}, bf16[10,4,4096]{2,1,0:T(4,128)(2,1)S(1)}, u32[]{:S(2)}, u32[]{:S(2)}) collective-permute-start(bf16[10,4,4096]{2,1,0:T(4,128)(2,1)} %own_ref.1), channel_id=1, source_target_pairs={{16,0},{32,16},{48,32},{64,48},{80,64},{96,80},{112,96},{128,112},... | collective-permute-start | bytes 983048 | tf_op jit(solution)/shard_map/ppermute | solution.py:161
  6.8 1.4 %fusion = (bf16[10,2,4096]{2,1,0:T(2,128)(2,1)S(1)}, bf16[10,2,4096]{2,1,0:T(2,128)(2,1)S(1)}) fusion(bf16[10,4,4096]{2,1,0:T(4,128)(2,1)} %own_ref.1), kind=kLoop, calls=%fused_computation.1 | loop fusion | bytes 655360 | tf_op jit(solution)/shard_map/slice | solution.py:166
  8.2 1.9 %collective-permute-start.3 = (bf16[10,2,4096]{2,1,0:T(2,128)(2,1)S(1)}, bf16[10,2,4096]{2,1,0:T(2,128)(2,1)S(1)}, u32[]{:S(2)}, u32[]{:S(2)}) collective-permute-start(bf16[10,2,4096]{2,1,0:T(2,128)(2,1)S(1)} %get-tuple-element.15), channel_id=1, source_target_pairs={{32,0},{48,16},{64,32},{80,48},{96,64},{112,80},{128,96},{144,112}... | collective-permute-start | bytes 491528 | tf_op jit(solution)/shard_map/ppermute | solution.py:161
  10.1 3.9 %collective-permute-start = (bf16[10,2,4096]{2,1,0:T(2,128)(2,1)S(1)}, bf16[10,2,4096]{2,1,0:T(2,128)(2,1)S(1)}, u32[]{:S(2)}, u32[]{:S(2)}) collective-permute-start(bf16[10,2,4096]{2,1,0:T(2,128)(2,1)S(1)} %get-tuple-element.16), channel_id=1, source_target_pairs={{0,32},{16,48},{32,64},{48,80},{64,96},{80,112},{96,128},{112,144}... | collective-permute-start | bytes 491528 | tf_op jit(solution)/shard_map/ppermute | solution.py:161
  14.1 3.2 %prep.1 = (bf16[1536,192]{1,0:T(8,128)(2,1)}, bf16[128,256]{1,0:T(8,128)(2,1)}, f32[768,128]{1,0:T(8,128)}, f32[16,128]{1,0:T(8,128)}, s32[32,128]{1,0:T(8,128)}) custom-call(s32[1]{0:T(128)} %bitcast.date_ref, s32[1]{0:T(128)} %bitcast.1.tile_ref, s32[12,192]{1,0:T(8,128)} %constant.13.clone.table_ref, bf16[10,128]{1,0:T(8,128)(2,1)} %lift_ref.1, ...), custom_call_target="tpu_custom_call" | custom-call | tf_op jit(solution)/shard_map/prep/pallas_call | solution.py:171
  17.3 0.0 collective-permute-done.3.p2_ref
  17.3 0.0 copy-start.2
  17.3 2.1 %collective-permute-done.m2_ref = bf16[10,2,4096]{2,1,0:T(2,128)(2,1)S(1)} collective-permute-done((bf16[10,2,4096]{2,1,0:T(2,128)(2,1)S(1)}, bf16[10,2,4096]{2,1,0:T(2,128)(2,1)S(1)}, u32[]{:S(2)}, u32[]{:S(2)}) %collective-permute-start) | collective-permute-done | bytes 163872 | tf_op jit(solution)/shard_map/ppermute | solution.py:161
  19.5 0.0 copy-start.3
  19.5 0.0 collective-permute-done.1.m1_ref
  19.5 0.0 copy-start
  19.5 0.0 collective-permute-done.2.p1_ref
  19.5 0.0 copy-start.1
  19.5 0.0 copy-done.2
  19.5 0.6 %copy-done.3 = bf16[10,2,4096]{2,1,0:T(2,128)(2,1)} copy-done((bf16[10,2,4096]{2,1,0:T(2,128)(2,1)}, bf16[10,2,4096]{2,1,0:T(2,128)(2,1)S(1)}, u32[]{:S(2)}) %copy-start.3) | copy-done | bytes 163864
  20.1 0.1 copy-done
  20.3 0.1 copy-done.1
  20.4 9.6 %encode.1 = f32[256,128]{1,0:T(8,128)} custom-call(bf16[10,2,4096]{2,1,0:T(2,128)(2,1)} %copy-done.3, bf16[10,4,4096]{2,1,0:T(4,128)(2,1)} %copy-done, bf16[10,4,4096]{2,1,0:T(4,128)(2,1)} %own_ref.1, bf16[10,4,4096]{2,1,0:T(4,128)(2,1)} %copy-done.1, bf16[10,2,4096]{2,1,0:T(2,128)(2,1)} %copy-done.2, bf16[1536,192]{1,0:T(8,128)(2,1)} %get-tuple-element.10.w0_ref, ...), custom_call_target="tpu_custom_call" | custom-call | tf_op jit(solution)/shard_map/encode/pallas_call | solution.py:186
  30.0 14.9 %all_to_all.9 = f32[16,16,128]{2,1,0:T(8,128)S(1)} all-to-all(f32[16,16,128]{2,1,0:T(8,128)} %bitcast.8), channel_id=1, replica_groups=mesh['date'=16,'tile'=16] {'tile'}, dimensions={0} | all-to-all | bytes 262144 | tf_op jit(solution)/shard_map/all_to_all | solution.py:194
  44.8 0.0 copy-start.4
  44.8 0.7 %copy-done.4 = f32[16,128]{1,0:T(8,128)S(1)} copy-done((f32[16,128]{1,0:T(8,128)S(1)}, f32[16,128]{1,0:T(8,128)}, u32[]{:S(2)}) %copy-start.4) | copy-done | bytes 8216
  45.5 0.6 %divide_bitcast_fusion = f32[1,16,128]{2,1,0:T(8,128)} fusion(f32[16,128]{1,0:T(8,128)S(1)} %reduce_sum.9, f32[16,128]{1,0:T(8,128)S(1)} %copy-done.4), kind=kLoop, calls=%fused_computation | loop fusion | flops 4096 | bytes 24576 | tf_op jit(solution)/shard_map/broadcast_in_dim | solution.py:196
  (1 shorter events, 0.0 us)
Async XLA Ops:
  0.0 19.5 %collective-permute-start.1 = (bf16[10,4,4096]{2,1,0:T(4,128)(2,1)}, bf16[10,4,4096]{2,1,0:T(4,128)(2,1)S(1)}, u32[]{:S(2)}, u32[]{:S(2)}) collective-permute-start(bf16[10,4,4096]{2,1,0:T(4,128)(2,1)} %own_ref.1), channel_id=1, source_target_pairs={{0,16},{16,32},{32,48},{48,64},{64,80},{80,96},{96,112},{112,128},... | collective-permute-start | bytes 983048 | tf_op jit(solution)/shard_map/ppermute | solution.py:161
  1.9 17.5 %collective-permute-start.2 = (bf16[10,4,4096]{2,1,0:T(4,128)(2,1)}, bf16[10,4,4096]{2,1,0:T(4,128)(2,1)S(1)}, u32[]{:S(2)}, u32[]{:S(2)}) collective-permute-start(bf16[10,4,4096]{2,1,0:T(4,128)(2,1)} %own_ref.1), channel_id=1, source_target_pairs={{16,0},{32,16},{48,32},{64,48},{80,64},{96,80},{112,96},{128,112},... | collective-permute-start | bytes 983048 | tf_op jit(solution)/shard_map/ppermute | solution.py:161
  8.2 9.1 %collective-permute-start.3 = (bf16[10,2,4096]{2,1,0:T(2,128)(2,1)S(1)}, bf16[10,2,4096]{2,1,0:T(2,128)(2,1)S(1)}, u32[]{:S(2)}, u32[]{:S(2)}) collective-permute-start(bf16[10,2,4096]{2,1,0:T(2,128)(2,1)S(1)} %get-tuple-element.15), channel_id=1, source_target_pairs={{32,0},{48,16},{64,32},{80,48},{96,64},{112,80},{128,96},{144,112}... | collective-permute-start | bytes 491528 | tf_op jit(solution)/shard_map/ppermute | solution.py:161
  10.1 9.3 %collective-permute-start = (bf16[10,2,4096]{2,1,0:T(2,128)(2,1)S(1)}, bf16[10,2,4096]{2,1,0:T(2,128)(2,1)S(1)}, u32[]{:S(2)}, u32[]{:S(2)}) collective-permute-start(bf16[10,2,4096]{2,1,0:T(2,128)(2,1)S(1)} %get-tuple-element.16), channel_id=1, source_target_pairs={{0,32},{16,48},{32,64},{48,80},{64,96},{80,112},{96,128},{112,144}... | collective-permute-start | bytes 491528 | tf_op jit(solution)/shard_map/ppermute | solution.py:161
  17.3 2.2 %copy-start.2 = (bf16[10,2,4096]{2,1,0:T(2,128)(2,1)}, bf16[10,2,4096]{2,1,0:T(2,128)(2,1)S(1)}, u32[]{:S(2)}) copy-start(bf16[10,2,4096]{2,1,0:T(2,128)(2,1)S(1)} %collective-permute-done.3.p2_ref) | copy-start | bytes 491524
  19.5 0.7 %copy-start.3 = (bf16[10,2,4096]{2,1,0:T(2,128)(2,1)}, bf16[10,2,4096]{2,1,0:T(2,128)(2,1)S(1)}, u32[]{:S(2)}) copy-start(bf16[10,2,4096]{2,1,0:T(2,128)(2,1)S(1)} %collective-permute-done.m2_ref) | copy-start | bytes 491524
  19.5 0.8 %copy-start = (bf16[10,4,4096]{2,1,0:T(4,128)(2,1)}, bf16[10,4,4096]{2,1,0:T(4,128)(2,1)S(1)}, u32[]{:S(2)}) copy-start(bf16[10,4,4096]{2,1,0:T(4,128)(2,1)S(1)} %collective-permute-done.1.m1_ref) | copy-start | bytes 983044
  19.5 0.9 %copy-start.1 = (bf16[10,4,4096]{2,1,0:T(4,128)(2,1)}, bf16[10,4,4096]{2,1,0:T(4,128)(2,1)S(1)}, u32[]{:S(2)}) copy-start(bf16[10,4,4096]{2,1,0:T(4,128)(2,1)S(1)} %collective-permute-done.2.p1_ref) | copy-start | bytes 983044
  44.8 0.7 %copy-start.4 = (f32[16,128]{1,0:T(8,128)S(1)}, f32[16,128]{1,0:T(8,128)}, u32[]{:S(2)}) copy-start(f32[16,128]{1,0:T(8,128)} %get-tuple-element.14) | copy-start | bytes 24580

commit v3 on v2

--- a/solution.py
+++ b/solution.py
@@ -12,6 +12,8 @@
 EPSILON = 1e-05
 SECTION = 48
 BLOCK = 1024
+VMEM_LIMIT = 32 * 2**20
+UNROLL = 4
 
 SECTIONS = ((-6, 2), (-4, 4), (0, 4), (4, 4), (8, 2))
 FIRST = (0, 1, 1, 2, 2, 3)
@@ -87,37 +89,72 @@
         )
 
 
-def main_kernel(m2_ref, m1_ref, own_ref, p1_ref, p2_ref, w0_ref, w1_ref, columns_ref,
-                ids_ref, out_ref, stack_ref, *, taps):
+def fill_stack(stack_ref, sections, refs, columns):
+    for place, (s, ref) in enumerate(zip(sections, refs)):
+        held = SECTIONS[s][1]
+        for b in range(ref.shape[0]):
+            start = place * SECTION + b * held
+            stack_ref[start : start + held, :] = ref[b, :, columns]
+
+
+def clear_stack(stack_ref, sections):
+    stack_ref[...] = jnp.zeros(stack_ref.shape, jnp.bfloat16)
+    row = lax.broadcasted_iota(jnp.int32, (16, BLOCK), 0)
+    ones = jnp.where(row == 8, 1.0, 0.0).astype(jnp.bfloat16)
+    for place, s in enumerate(sections):
+        if SECTIONS[s][1] == 4:
+            stack_ref[place * SECTION + 32 : (place + 1) * SECTION, :] = ones
+
+
+def first_layer(stack_ref, place, w0_ref, lo, hi):
+    part = stack_ref[place * SECTION : (place + 2) * SECTION, :]
+    mixed = jnp.dot(w0_ref[lo * 256 : hi * 256, :], jnp.concatenate([part, part], axis=0),
+                    preferred_element_type=jnp.float32)
+    mixed = jnp.maximum(mixed, 0.0)
+    return [
+        (mixed[v * 256 : v * 256 + 128] + mixed[v * 256 + 128 : (v + 1) * 256]).astype(jnp.bfloat16)
+        for v in range(hi - lo)
+    ]
+
+
+def blocks(pixels, step):
+    def run(i, carry):
+        step(i, pl.ds(pl.multiple_of(i * BLOCK, BLOCK), BLOCK))
+        return carry
+
+    lax.fori_loop(0, pixels // BLOCK, run, 0, unroll=UNROLL)
+
+
+def middle_kernel(m1_ref, own_ref, p1_ref, w0_ref, out_ref, stack_ref):
+    sections = (1, 2, 3)
+    clear_stack(stack_ref, sections)
+
+    def step(i, columns):
+        fill_stack(stack_ref, sections, (m1_ref, own_ref, p1_ref), columns)
+        pooled = first_layer(stack_ref, 0, w0_ref, 1, 3) + first_layer(stack_ref, 1, w0_ref, 3, 5)
+        for v in range(4):
+            out_ref[v * 128 : (v + 1) * 128, columns] = pooled[v]
+
+    blocks(own_ref.shape[2], step)
+
+
+def main_kernel(m2_ref, m1_ref, p1_ref, p2_ref, w0_ref, w1_ref, columns_ref, ids_ref, middle_ref,
+                out_ref, stack_ref, *, taps):
     f32, bf16 = jnp.float32, jnp.bfloat16
-    stack_ref[...] = jnp.zeros(stack_ref.shape, bf16)
-    for s in (1, 2, 3):
-        row = lax.broadcasted_iota(jnp.int32, (16, BLOCK), 0)
-        stack_ref[s * SECTION + 32 : s * SECTION + 48, :] = jnp.where(row == 8, 1.0, 0.0).astype(bf16)
+    sections = (0, 1, 3, 4)
+    clear_stack(stack_ref, sections)
+    out_ref[...] = jnp.zeros(out_ref.shape, f32)
 
     def column(k):
         return jnp.concatenate([columns_ref[k * 128 : (k + 1) * 128, :]] * (BLOCK // 128), axis=1)
 
-    def pooled_pair(values):
-        return (jnp.maximum(values[:128], 0.0) + jnp.maximum(values[128:], 0.0)).astype(bf16)
-
-    def stacked(section):
-        part = stack_ref[section * SECTION : (section + 2) * SECTION, :]
-        return jnp.concatenate([part, part], axis=0)
-
-    def step(i, total):
-        columns = pl.ds(pl.multiple_of(i * BLOCK, BLOCK), BLOCK)
-        for s, ref in enumerate((m2_ref, m1_ref, own_ref, p1_ref, p2_ref)):
-            held = SECTIONS[s][1]
-            for b in range(ref.shape[0]):
-                start = s * SECTION + b * held
-                stack_ref[start : start + held, :] = ref[b, :, columns]
-        pooled = []
-        for section, lo, hi in ((0, 0, 1), (1, 1, 3), (2, 3, 5), (3, 5, 6)):
-            mixed = jnp.dot(w0_ref[lo * 256 : hi * 256, :], stacked(section),
-                            preferred_element_type=f32)
-            for v in range(hi - lo):
-                pooled.append(pooled_pair(mixed[v * 256 : (v + 1) * 256]))
+    def step(i, columns):
+        fill_stack(stack_ref, sections, (m2_ref, m1_ref, p1_ref, p2_ref), columns)
+        pooled = (
+            first_layer(stack_ref, 0, w0_ref, 0, 1)
+            + [middle_ref[v * 128 : (v + 1) * 128, columns] for v in range(4)]
+            + first_layer(stack_ref, 2, w0_ref, 5, 6)
+        )
         halves = []
         for e in range(2):
             spread = column(0) * pooled[e].astype(f32)
@@ -137,13 +174,11 @@
             ],
             axis=1,
         )
-        return total + lax.dot_general(
+        out_ref[...] += lax.dot_general(
             member, features, (((1,), (1,)), ((), ())), preferred_element_type=f32
         )
 
-    out_ref[...] = lax.fori_loop(
-        0, own_ref.shape[2] // BLOCK, step, jnp.zeros(out_ref.shape, f32)
-    )
+    blocks(m1_ref.shape[2], step)
 
 
 def local(imagery, owner, parcel_local, lift_weight, depth_weight, point_weight, bn_mean, bn_var,
@@ -165,32 +200,50 @@
     before_two = shifted(imagery[:, 2:4], 2)
     after_two = shifted(imagery[:, 0:2], -2)
 
+    def far(*arrays):
+        return [pltpu.with_memory_space_constraint(x, pltpu.HBM) for x in arrays]
+
     table = jnp.asarray(column_table(bands, taps))
     vmem = pl.BlockSpec(memory_space=pltpu.VMEM)
     smem = pl.BlockSpec(memory_space=pltpu.SMEM)
     w0, w1, columns, counts, ids = pl.pallas_call(
         functools.partial(prep_kernel, dates=dates),
         out_shape=(
-            jax.ShapeDtypeStruct((12 * channels, 4 * SECTION), jnp.bfloat16),
-            jax.ShapeDtypeStruct((channels, 2 * channels), jnp.bfloat16),
-            jax.ShapeDtypeStruct(((taps + 1) * channels, channels), jnp.float32),
-            jax.ShapeDtypeStruct((PARC_DEV, channels), jnp.float32),
-            jax.ShapeDtypeStruct((pix_dev // 128, 128), jnp.int32),
+            pltpu.VMEM((12 * channels, 4 * SECTION), jnp.bfloat16),
+            pltpu.VMEM((channels, 2 * channels), jnp.bfloat16),
+            pltpu.VMEM(((taps + 1) * channels, channels), jnp.float32),
+            pltpu.VMEM((PARC_DEV, channels), jnp.float32),
+            pltpu.VMEM((pix_dev // 128, 128), jnp.int32),
         ),
         in_specs=[smem] * 2 + [vmem] * 10,
         out_specs=(vmem,) * 5,
+        compiler_params=pltpu.CompilerParams(vmem_limit_bytes=VMEM_LIMIT),
         name="prep",
-    )(date_index.reshape(1), tile_index.reshape(1), table, lift_weight,
-      depth_weight.transpose(1, 0, 2), point_weight, bn_mean, bn_var, bn_gain, bn_shift,
-      owner.reshape(-1, 128), parcel_local.reshape(-1, 128))
+    )(date_index.reshape(1), tile_index.reshape(1), *far(
+        table, lift_weight, depth_weight.transpose(1, 0, 2), point_weight, bn_mean, bn_var,
+        bn_gain, bn_shift, owner.reshape(-1, 128), parcel_local.reshape(-1, 128)))
+
+    def near(*arrays):
+        return [pltpu.with_memory_space_constraint(x, pltpu.VMEM) for x in arrays]
+
+    middle = pl.pallas_call(
+        middle_kernel,
+        out_shape=pltpu.VMEM((4 * channels, pix_dev), jnp.bfloat16),
+        in_specs=[vmem] * 4,
+        out_specs=vmem,
+        scratch_shapes=[pltpu.VMEM((3 * SECTION, BLOCK), jnp.bfloat16)],
+        compiler_params=pltpu.CompilerParams(vmem_limit_bytes=VMEM_LIMIT),
+        name="middle",
+    )(*near(before, imagery, after, w0))
     sums = pl.pallas_call(
         functools.partial(main_kernel, taps=taps),
         out_shape=jax.ShapeDtypeStruct((tiles * PARC_DEV, channels), jnp.float32),
         in_specs=[vmem] * 9,
         out_specs=vmem,
-        scratch_shapes=[pltpu.VMEM((5 * SECTION, BLOCK), jnp.bfloat16)],
+        scratch_shapes=[pltpu.VMEM((4 * SECTION, BLOCK), jnp.bfloat16)],
+        compiler_params=pltpu.CompilerParams(vmem_limit_bytes=VMEM_LIMIT),
         name="encode",
-    )(before_two, before, imagery, after, after_two, w0, w1, columns, ids)
+    )(*near(before_two, before, after, after_two, w0, w1, columns, ids, middle))
     arrived = lax.all_to_all(sums, "tile", split_axis=0, concat_axis=0, tiled=True)
     total = jnp.sum(arrived.reshape(tiles, PARC_DEV, channels), axis=0)
     return (total / jnp.maximum(counts, 1.0))[None]

time: 46.5 us -> 41 us (0.88)
  the two profiles are of different devices: /device:TPU:128 before, /device:TPU:96 now
where the time goes in v3:
time: 41 us; the launch traced here: 40.7 us
  blocking collectives  14.7 us (36%)
  starting transfers between devices  13.7 us (33%)
  Pallas kernels  9.19 us (22%)
  local copies, waits for them, and re-layouts  2.4 us (6%)
  other arithmetic  0.63 us (2%)
    all_to_all x1, blocking collectives, local(): lax.all_to_all(sums, 'tile', split_axis=0, concat_axis=0, tiled=True)  14.7 us
    ppermute x4, starting transfers between devices, shifted(): return lax.ppermute(value, 'date', pairs)  13.7 us
    pallas_call x1, Pallas kernels, local(): pl.pallas_call(functools.partial(main_kernel, taps=taps), out_shape=jax.S...  4.45 us
    pallas_call x1, Pallas kernels, local(): pl.pallas_call(middle_kernel, out_shape=pltpu.VMEM((4 * channels, pix_dev...  2.44 us
    pallas_call x1, Pallas kernels, local(): pl.pallas_call(functools.partial(prep_kernel, dates=dates), out_shape=(pl...  2.3 us
    slice x1, local copies, waits for them, and re-layouts, local(): after_two = shifted(imagery[:, 0:2], -2)  1.43 us
    unnamed x2, local copies, waits for them, and re-layouts  0.97 us
  transfers between devices with their start and end apart: 4, of which 0 were waited for; matrix products, arithmetic and copies ran while one was open for 4% of the time, Pallas kernels for 12%

profile of v3, /device:TPU:96, one launch (start us, length us, event | category | flops | bytes accessed | tf_op | source)
XLA Modules:
  0.0 40.7 jit_solution(8682038923530214103)
XLA Ops:
  0.0 1.9 %collective-permute-start.1 = (bf16[10,4,4096]{2,1,0:T(4,128)(2,1)}, bf16[10,4,4096]{2,1,0:T(4,128)(2,1)S(1)}, u32[]{:S(2)}, u32[]{:S(2)}) collective-permute-start(bf16[10,4,4096]{2,1,0:T(4,128)(2,1)} %own_ref.1), channel_id=1, source_target_pairs={{0,16},{16,32},{32,48},{48,64},{64,80},{80,96},{96,112},{112,128},... | collective-permute-start | bytes 983048 | tf_op jit(solution)/shard_map/ppermute | solution.py:196
  1.9 3.6 %collective-permute-start.2 = (bf16[10,4,4096]{2,1,0:T(4,128)(2,1)}, bf16[10,4,4096]{2,1,0:T(4,128)(2,1)S(1)}, u32[]{:S(2)}, u32[]{:S(2)}) collective-permute-start(bf16[10,4,4096]{2,1,0:T(4,128)(2,1)} %own_ref.1), channel_id=1, source_target_pairs={{16,0},{32,16},{48,32},{64,48},{80,64},{96,80},{112,96},{128,112},... | collective-permute-start | bytes 983048 | tf_op jit(solution)/shard_map/ppermute | solution.py:196
  5.6 1.4 %fusion = (bf16[10,2,4096]{2,1,0:T(2,128)(2,1)S(1)}, bf16[10,2,4096]{2,1,0:T(2,128)(2,1)S(1)}) fusion(bf16[10,4,4096]{2,1,0:T(4,128)(2,1)} %own_ref.1), kind=kLoop, calls=%fused_computation.1 | loop fusion | bytes 655360 | tf_op jit(solution)/shard_map/slice | solution.py:201
  7.0 2.0 %collective-permute-start.3 = (bf16[10,2,4096]{2,1,0:T(2,128)(2,1)S(1)}, bf16[10,2,4096]{2,1,0:T(2,128)(2,1)S(1)}, u32[]{:S(2)}, u32[]{:S(2)}) collective-permute-start(bf16[10,2,4096]{2,1,0:T(2,128)(2,1)S(1)} %get-tuple-element.15), channel_id=1, source_target_pairs={{32,0},{48,16},{64,32},{80,48},{96,64},{112,80},{128,96},{144,112}... | collective-permute-start | bytes 491528 | tf_op jit(solution)/shard_map/ppermute | solution.py:196
  9.0 6.2 %collective-permute-start = (bf16[10,2,4096]{2,1,0:T(2,128)(2,1)S(1)}, bf16[10,2,4096]{2,1,0:T(2,128)(2,1)S(1)}, u32[]{:S(2)}, u32[]{:S(2)}) collective-permute-start(bf16[10,2,4096]{2,1,0:T(2,128)(2,1)S(1)} %get-tuple-element.16), channel_id=1, source_target_pairs={{0,32},{16,48},{32,64},{48,80},{64,96},{80,112},{96,128},{112,144}... | collective-permute-start | bytes 491528 | tf_op jit(solution)/shard_map/ppermute | solution.py:196
  15.2 2.3 %prep.1 = (bf16[1536,192]{1,0:T(8,128)(2,1)S(1)}, bf16[128,256]{1,0:T(8,128)(2,1)S(1)}, f32[768,128]{1,0:T(8,128)S(1)}, f32[16,128]{1,0:T(8,128)S(1)}, s32[32,128]{1,0:T(8,128)S(1)}) custom-call(s32[1]{0:T(128)} %bitcast.date_ref, s32[1]{0:T(128)} %bitcast.1.tile_ref, s32[12,192]{1,0:T(8,128)} %constant.13.clone.table_ref, bf16[10,128]{1,0:T(8,128)(2,1)} %lift_ref.1, ...), custom_call_target="tpu_custom_call" | custom-call | tf_op jit(solution)/shard_map/prep/pallas_call | solution.py:209
  17.5 0.0 collective-permute-done.1.m1_ref
  17.5 0.0 collective-permute-done.2.p1_ref
  17.5 0.0 copy-start
  17.5 1.0 %copy-done = bf16[10,4,4096]{2,1,0:T(4,128)(2,1)S(1)} copy-done((bf16[10,4,4096]{2,1,0:T(4,128)(2,1)S(1)}, bf16[10,4,4096]{2,1,0:T(4,128)(2,1)}, u32[]{:S(2)}) %copy-start) | copy-done | bytes 327704
  18.5 2.4 %middle.1.middle_ref = bf16[512,4096]{1,0:T(8,128)(2,1)S(1)} custom-call(bf16[10,4,4096]{2,1,0:T(4,128)(2,1)S(1)} %collective-permute-done.1.m1_ref, bf16[10,4,4096]{2,1,0:T(4,128)(2,1)S(1)} %copy-done, bf16[10,4,4096]{2,1,0:T(4,128)(2,1)S(1)} %collective-permute-done.2.p1_ref, bf16[1536,192]{1,0:T(8,128)(2,1)S(1)} %get-tuple-element.10.w0_ref), custom_call_target="tpu_custom_call" | custom-call | tf_op jit(solution)/shard_map/middle/pallas_call | solution.py:229
  20.9 0.0 collective-permute-done.3.p2_ref
  20.9 0.0 collective-permute-done.m2_ref
  21.0 4.5 %encode.1 = f32[256,128]{1,0:T(8,128)S(1)} custom-call(bf16[10,2,4096]{2,1,0:T(2,128)(2,1)S(1)} %collective-permute-done.m2_ref, bf16[10,4,4096]{2,1,0:T(4,128)(2,1)S(1)} %collective-permute-done.1.m1_ref, bf16[10,4,4096]{2,1,0:T(4,128)(2,1)S(1)} %collective-permute-done.2.p1_ref, bf16[10,2,4096]{2,1,0:T(2,128)(2,1)S(1)} %collective-permute-done.3.p2_ref, ...), custom_call_target="tpu_custom_call" | custom-call | tf_op jit(solution)/shard_map/encode/pallas_call | solution.py:238
  25.4 14.7 %all_to_all.9 = f32[16,16,128]{2,1,0:T(8,128)S(1)} all-to-all(f32[16,16,128]{2,1,0:T(8,128)S(1)} %bitcast.8), channel_id=1, replica_groups=mesh['date'=16,'tile'=16] {'tile'}, dimensions={0} | all-to-all | bytes 262144 | tf_op jit(solution)/shard_map/all_to_all | solution.py:247
  40.1 0.6 %divide_bitcast_fusion = f32[1,16,128]{2,1,0:T(8,128)} fusion(f32[16,128]{1,0:T(8,128)S(1)} %reduce_sum.9, f32[16,128]{1,0:T(8,128)S(1)} %get-tuple-element.14), kind=kLoop, calls=%fused_computation | loop fusion | flops 4096 | bytes 24576 | tf_op jit(solution)/shard_map/broadcast_in_dim | solution.py:249
  (1 shorter events, 0.0 us)
Async XLA Ops:
  0.0 17.5 %collective-permute-start.1 = (bf16[10,4,4096]{2,1,0:T(4,128)(2,1)}, bf16[10,4,4096]{2,1,0:T(4,128)(2,1)S(1)}, u32[]{:S(2)}, u32[]{:S(2)}) collective-permute-start(bf16[10,4,4096]{2,1,0:T(4,128)(2,1)} %own_ref.1), channel_id=1, source_target_pairs={{0,16},{16,32},{32,48},{48,64},{64,80},{80,96},{96,112},{112,128},... | collective-permute-start | bytes 983048 | tf_op jit(solution)/shard_map/ppermute | solution.py:196
  1.9 15.6 %collective-permute-start.2 = (bf16[10,4,4096]{2,1,0:T(4,128)(2,1)}, bf16[10,4,4096]{2,1,0:T(4,128)(2,1)S(1)}, u32[]{:S(2)}, u32[]{:S(2)}) collective-permute-start(bf16[10,4,4096]{2,1,0:T(4,128)(2,1)} %own_ref.1), channel_id=1, source_target_pairs={{16,0},{32,16},{48,32},{64,48},{80,64},{96,80},{112,96},{128,112},... | collective-permute-start | bytes 983048 | tf_op jit(solution)/shard_map/ppermute | solution.py:196
  7.0 13.9 %collective-permute-start.3 = (bf16[10,2,4096]{2,1,0:T(2,128)(2,1)S(1)}, bf16[10,2,4096]{2,1,0:T(2,128)(2,1)S(1)}, u32[]{:S(2)}, u32[]{:S(2)}) collective-permute-start(bf16[10,2,4096]{2,1,0:T(2,128)(2,1)S(1)} %get-tuple-element.15), channel_id=1, source_target_pairs={{32,0},{48,16},{64,32},{80,48},{96,64},{112,80},{128,96},{144,112}... | collective-permute-start | bytes 491528 | tf_op jit(solution)/shard_map/ppermute | solution.py:196
  9.0 11.9 %collective-permute-start = (bf16[10,2,4096]{2,1,0:T(2,128)(2,1)S(1)}, bf16[10,2,4096]{2,1,0:T(2,128)(2,1)S(1)}, u32[]{:S(2)}, u32[]{:S(2)}) collective-permute-start(bf16[10,2,4096]{2,1,0:T(2,128)(2,1)S(1)} %get-tuple-element.16), channel_id=1, source_target_pairs={{0,32},{16,48},{32,64},{48,80},{64,96},{80,112},{96,128},{112,144}... | collective-permute-start | bytes 491528 | tf_op jit(solution)/shard_map/ppermute | solution.py:196
  17.5 1.0 %copy-start = (bf16[10,4,4096]{2,1,0:T(4,128)(2,1)S(1)}, bf16[10,4,4096]{2,1,0:T(4,128)(2,1)}, u32[]{:S(2)}) copy-start(bf16[10,4,4096]{2,1,0:T(4,128)(2,1)} %own_ref.1) | copy-start | bytes 983044

commit v4 on v3

--- a/solution.py
+++ b/solution.py
@@ -92,9 +92,13 @@
 def fill_stack(stack_ref, sections, refs, columns):
     for place, (s, ref) in enumerate(zip(sections, refs)):
         held = SECTIONS[s][1]
-        for b in range(ref.shape[0]):
+        for b in range(ref[1].shape[0]):
             start = place * SECTION + b * held
-            stack_ref[start : start + held, :] = ref[b, :, columns]
+            stack_ref[start : start + held, :] = (
+                ref[1][b, :, columns]
+                if ref[0] is None
+                else jnp.where(ref[0], ref[1][b, :, columns], ref[2][b, :, columns])
+            )
 
 
 def clear_stack(stack_ref, sections):
@@ -125,12 +129,16 @@
     lax.fori_loop(0, pixels // BLOCK, run, 0, unroll=UNROLL)
 
 
-def middle_kernel(m1_ref, own_ref, p1_ref, w0_ref, out_ref, stack_ref):
+def middle_kernel(date_ref, partner_ref, own_ref, across_ref, w0_ref, out_ref, stack_ref):
     sections = (1, 2, 3)
+    core_odd = date_ref[0] % 2 == 1
+    held = (
+        (core_odd, partner_ref, across_ref), (None, own_ref), (core_odd, across_ref, partner_ref)
+    )
     clear_stack(stack_ref, sections)
 
     def step(i, columns):
-        fill_stack(stack_ref, sections, (m1_ref, own_ref, p1_ref), columns)
+        fill_stack(stack_ref, sections, held, columns)
         pooled = first_layer(stack_ref, 0, w0_ref, 1, 3) + first_layer(stack_ref, 1, w0_ref, 3, 5)
         for v in range(4):
             out_ref[v * 128 : (v + 1) * 128, columns] = pooled[v]
@@ -138,10 +146,16 @@
     blocks(own_ref.shape[2], step)
 
 
-def main_kernel(m2_ref, m1_ref, p1_ref, p2_ref, w0_ref, w1_ref, columns_ref, ids_ref, middle_ref,
-                out_ref, stack_ref, *, taps):
+def main_kernel(date_ref, even_ref, odd_ref, partner_ref, across_ref, w0_ref, w1_ref, columns_ref,
+                ids_ref, middle_ref, out_ref, stack_ref, *, taps):
     f32, bf16 = jnp.float32, jnp.bfloat16
     sections = (0, 1, 3, 4)
+    core_odd = date_ref[0] % 2 == 1
+    chip_odd = date_ref[0] // 2 % 2 == 1
+    refs = (
+        (chip_odd, even_ref, odd_ref), (core_odd, partner_ref, across_ref),
+        (core_odd, across_ref, partner_ref), (chip_odd, odd_ref, even_ref),
+    )
     clear_stack(stack_ref, sections)
     out_ref[...] = jnp.zeros(out_ref.shape, f32)
 
@@ -149,7 +163,7 @@
         return jnp.concatenate([columns_ref[k * 128 : (k + 1) * 128, :]] * (BLOCK // 128), axis=1)
 
     def step(i, columns):
-        fill_stack(stack_ref, sections, (m2_ref, m1_ref, p1_ref, p2_ref), columns)
+        fill_stack(stack_ref, sections, refs, columns)
         pooled = (
             first_layer(stack_ref, 0, w0_ref, 0, 1)
             + [middle_ref[v * 128 : (v + 1) * 128, columns] for v in range(4)]
@@ -178,7 +192,7 @@
             member, features, (((1,), (1,)), ((), ())), preferred_element_type=f32
         )
 
-    blocks(m1_ref.shape[2], step)
+    blocks(across_ref.shape[2], step)
 
 
 def local(imagery, owner, parcel_local, lift_weight, depth_weight, point_weight, bn_mean, bn_var,
@@ -191,14 +205,21 @@
     channels = lift_weight.shape[1]
     taps = depth_weight.shape[1]
 
-    def shifted(value, by):
-        pairs = [(d, d + by) for d in range(dates) if 0 <= d + by < dates]
-        return lax.ppermute(value, "date", pairs)
-
-    before = shifted(imagery, 1)
-    after = shifted(imagery, -1)
-    before_two = shifted(imagery[:, 2:4], 2)
-    after_two = shifted(imagery[:, 0:2], -2)
+    every = range(dates)
+    partner = [(d, d ^ 1) for d in every]
+    across = [(d, d + 1 if d % 2 else d - 1) for d in every]
+    even_pairs = [(d, d - 2 if d // 2 % 2 else d + 2) for d in every]
+    odd_pairs = [(d, d + 2 if d // 2 % 2 else d - 2) for d in every]
+
+    def swapped(value, pairs):
+        return lax.ppermute(value, "date", [(d, t) for d, t in pairs if 0 <= t < dates])
+
+    by_across = swapped(imagery, across)
+    by_partner = swapped(imagery, partner)
+    chip_odd = date_index // 2 % 2 == 1
+    first, last = imagery[:, 0:2], imagery[:, 2:4]
+    by_even = swapped(jnp.where(chip_odd, first, last), even_pairs)
+    by_odd = swapped(jnp.where(chip_odd, last, first), odd_pairs)
 
     def far(*arrays):
         return [pltpu.with_memory_space_constraint(x, pltpu.HBM) for x in arrays]
@@ -229,21 +250,22 @@
     middle = pl.pallas_call(
         middle_kernel,
         out_shape=pltpu.VMEM((4 * channels, pix_dev), jnp.bfloat16),
-        in_specs=[vmem] * 4,
+        in_specs=[smem] + [vmem] * 4,
         out_specs=vmem,
         scratch_shapes=[pltpu.VMEM((3 * SECTION, BLOCK), jnp.bfloat16)],
         compiler_params=pltpu.CompilerParams(vmem_limit_bytes=VMEM_LIMIT),
         name="middle",
-    )(*near(before, imagery, after, w0))
+    )(date_index.reshape(1), *near(by_partner, imagery, by_across, w0))
     sums = pl.pallas_call(
         functools.partial(main_kernel, taps=taps),
         out_shape=jax.ShapeDtypeStruct((tiles * PARC_DEV, channels), jnp.float32),
-        in_specs=[vmem] * 9,
+        in_specs=[smem] + [vmem] * 9,
         out_specs=vmem,
         scratch_shapes=[pltpu.VMEM((4 * SECTION, BLOCK), jnp.bfloat16)],
         compiler_params=pltpu.CompilerParams(vmem_limit_bytes=VMEM_LIMIT),
         name="encode",
-    )(*near(before_two, before, after, after_two, w0, w1, columns, ids, middle))
+    )(date_index.reshape(1),
+      *near(by_even, by_odd, by_partner, by_across, w0, w1, columns, ids, middle))
     arrived = lax.all_to_all(sums, "tile", split_axis=0, concat_axis=0, tiled=True)
     total = jnp.sum(arrived.reshape(tiles, PARC_DEV, channels), axis=0)
     return (total / jnp.maximum(counts, 1.0))[None]

time: 41 us -> 37.2 us (0.907)
  the two profiles are of different devices: /device:TPU:96 before, /device:TPU:1 now
where the time goes in v4:
time: 37.2 us; the launch traced here: 37 us
  blocking collectives  14 us (38%)
  starting transfers between devices  10.2 us (27%)
  Pallas kernels  9.59 us (26%)
  other arithmetic  2.1 us (6%)
  local copies, waits for them, and re-layouts  0.97 us (3%)
    all_to_all x1, blocking collectives, local(): lax.all_to_all(sums, 'tile', split_axis=0, concat_axis=0, tiled=True)  14 us
    ppermute x4, starting transfers between devices, swapped(): lax.ppermute(value, 'date', [(d, t) for d, t in pairs if 0 <= t < dates])  10.2 us
    pallas_call x1, Pallas kernels, local(): pl.pallas_call(functools.partial(main_kernel, taps=taps), out_shape=jax.S...  4.82 us
    pallas_call x1, Pallas kernels, local(): pl.pallas_call(middle_kernel, out_shape=pltpu.VMEM((4 * channels, pix_dev...  2.48 us
    pallas_call x1, Pallas kernels, local(): pl.pallas_call(functools.partial(prep_kernel, dates=dates), out_shape=(pl...  2.29 us
    select_n x1, other arithmetic, local(): by_odd = swapped(jnp.where(chip_odd, last, first), odd_pairs)  1.47 us
    unnamed x2, local copies, waits for them, and re-layouts  0.97 us
  transfers between devices with their start and end apart: 4, of which 0 were waited for; matrix products, arithmetic and copies ran while one was open for 4% of the time, Pallas kernels for 13%

profile of v4, /device:TPU:1, one launch (start us, length us, event | category | flops | bytes accessed | tf_op | source)
XLA Modules:
  0.0 37.0 jit_solution(6840353107245131380)
XLA Ops:
  0.0 3.2 %collective-permute-start.2 = (bf16[10,4,4096]{2,1,0:T(4,128)(2,1)}, bf16[10,4,4096]{2,1,0:T(4,128)(2,1)S(1)}, u32[]{:S(2)}, u32[]{:S(2)}) collective-permute-start(bf16[10,4,4096]{2,1,0:T(4,128)(2,1)} %own_ref.1), channel_id=1, source_target_pairs={{0,16},{16,0},{32,48},{48,32},{64,80},{80,64},{96,112},{112,96},{1... | collective-permute-start | bytes 983048 | tf_op jit(solution)/shard_map/ppermute | solution.py:215
  3.2 1.9 %collective-permute-start.3 = (bf16[10,4,4096]{2,1,0:T(4,128)(2,1)}, bf16[10,4,4096]{2,1,0:T(4,128)(2,1)S(1)}, u32[]{:S(2)}, u32[]{:S(2)}) collective-permute-start(bf16[10,4,4096]{2,1,0:T(4,128)(2,1)} %own_ref.1), channel_id=1, source_target_pairs={{16,32},{32,16},{48,64},{64,48},{80,96},{96,80},{112,128},{128,112... | collective-permute-start | bytes 983048 | tf_op jit(solution)/shard_map/ppermute | solution.py:215
  5.2 1.5 %broadcast_select_fusion = (bf16[10,2,4096]{2,1,0:T(2,128)(2,1)S(1)}, bf16[10,2,4096]{2,1,0:T(2,128)(2,1)S(1)}) fusion(pred[]{:T(512)S(6)} %eq.5, bf16[10,4,4096]{2,1,0:T(4,128)(2,1)} %own_ref.1), kind=kLoop, calls=%fused_computation | loop fusion | flops 163840 | bytes 655361 | tf_op jit(solution)/shard_map/jit(_where)/select_n | solution.py:222
  6.7 0.7 %collective-permute-start.1 = (bf16[10,2,4096]{2,1,0:T(2,128)(2,1)S(1)}, bf16[10,2,4096]{2,1,0:T(2,128)(2,1)S(1)}, u32[]{:S(2)}, u32[]{:S(2)}) collective-permute-start(bf16[10,2,4096]{2,1,0:T(2,128)(2,1)S(1)} %get-tuple-element.15), channel_id=1, source_target_pairs={{32,64},{48,80},{64,32},{80,48},{96,128},{112,144},{128,96},{144,1... | collective-permute-start | bytes 491528 | tf_op jit(solution)/shard_map/ppermute | solution.py:215
  7.3 4.4 %collective-permute-start = (bf16[10,2,4096]{2,1,0:T(2,128)(2,1)S(1)}, bf16[10,2,4096]{2,1,0:T(2,128)(2,1)S(1)}, u32[]{:S(2)}, u32[]{:S(2)}) collective-permute-start(bf16[10,2,4096]{2,1,0:T(2,128)(2,1)S(1)} %get-tuple-element.16), channel_id=1, source_target_pairs={{0,32},{16,48},{32,0},{48,16},{64,96},{80,112},{96,64},{112,80},{1... | collective-permute-start | bytes 491528 | tf_op jit(solution)/shard_map/ppermute | solution.py:215
  11.7 2.3 %prep.1 = (bf16[1536,192]{1,0:T(8,128)(2,1)S(1)}, bf16[128,256]{1,0:T(8,128)(2,1)S(1)}, f32[768,128]{1,0:T(8,128)S(1)}, f32[16,128]{1,0:T(8,128)S(1)}, s32[32,128]{1,0:T(8,128)S(1)}) custom-call(s32[1]{0:T(128)} %bitcast.date_ref, s32[1]{0:T(128)} %bitcast.1.tile_ref, s32[12,192]{1,0:T(8,128)} %constant.38.clone.table_ref, bf16[10,128]{1,0:T(8,128)(2,1)} %lift_ref.1, ...), custom_call_target="tpu_custom_call" | custom-call | tf_op jit(solution)/shard_map/prep/pallas_call | solution.py:230
  14.0 0.0 collective-permute-done.2.partner_ref
  14.0 0.0 collective-permute-done.3.across_ref
  14.0 0.0 copy-start
  14.0 1.0 %copy-done = bf16[10,4,4096]{2,1,0:T(4,128)(2,1)S(1)} copy-done((bf16[10,4,4096]{2,1,0:T(4,128)(2,1)S(1)}, bf16[10,4,4096]{2,1,0:T(4,128)(2,1)}, u32[]{:S(2)}) %copy-start) | copy-done | bytes 327704
  15.0 2.5 %middle.1.middle_ref = bf16[512,4096]{1,0:T(8,128)(2,1)S(1)} custom-call(s32[1]{0:T(128)} %bitcast.date_ref, bf16[10,4,4096]{2,1,0:T(4,128)(2,1)S(1)} %collective-permute-done.2.partner_ref, bf16[10,4,4096]{2,1,0:T(4,128)(2,1)S(1)} %copy-done, bf16[10,4,4096]{2,1,0:T(4,128)(2,1)S(1)} %collective-permute-done.3.across_ref, ...), custom_call_target="tpu_custom_call" | custom-call | tf_op jit(solution)/shard_map/middle/pallas_call | solution.py:250
  17.5 0.0 collective-permute-done.1.odd_ref
  17.5 0.0 collective-permute-done.even_ref
  17.5 4.8 %encode.1 = f32[256,128]{1,0:T(8,128)S(1)} custom-call(s32[1]{0:T(128)} %bitcast.date_ref, bf16[10,2,4096]{2,1,0:T(2,128)(2,1)S(1)} %collective-permute-done.even_ref, bf16[10,2,4096]{2,1,0:T(2,128)(2,1)S(1)} %collective-permute-done.1.odd_ref, bf16[10,4,4096]{2,1,0:T(4,128)(2,1)S(1)} %collective-permute-done.2.partner_ref, ...), custom_call_target="tpu_custom_call" | custom-call | tf_op jit(solution)/shard_map/encode/pallas_call | solution.py:259
  22.3 14.0 %all_to_all.9 = f32[16,16,128]{2,1,0:T(8,128)S(1)} all-to-all(f32[16,16,128]{2,1,0:T(8,128)S(1)} %bitcast.8), channel_id=1, replica_groups=mesh['date'=16,'tile'=16] {'tile'}, dimensions={0} | all-to-all | bytes 262144 | tf_op jit(solution)/shard_map/all_to_all | solution.py:269
  36.4 0.6 %divide_bitcast_fusion = f32[1,16,128]{2,1,0:T(8,128)} fusion(f32[16,128]{1,0:T(8,128)S(1)} %reduce_sum.9, f32[16,128]{1,0:T(8,128)S(1)} %get-tuple-element.14), kind=kLoop, calls=%fused_computation.2 | loop fusion | flops 4096 | bytes 24576 | tf_op jit(solution)/shard_map/broadcast_in_dim | solution.py:271
  (1 shorter events, 0.0 us)
Async XLA Ops:
  0.0 14.0 %collective-permute-start.2 = (bf16[10,4,4096]{2,1,0:T(4,128)(2,1)}, bf16[10,4,4096]{2,1,0:T(4,128)(2,1)S(1)}, u32[]{:S(2)}, u32[]{:S(2)}) collective-permute-start(bf16[10,4,4096]{2,1,0:T(4,128)(2,1)} %own_ref.1), channel_id=1, source_target_pairs={{0,16},{16,0},{32,48},{48,32},{64,80},{80,64},{96,112},{112,96},{1... | collective-permute-start | bytes 983048 | tf_op jit(solution)/shard_map/ppermute | solution.py:215
  3.2 10.8 %collective-permute-start.3 = (bf16[10,4,4096]{2,1,0:T(4,128)(2,1)}, bf16[10,4,4096]{2,1,0:T(4,128)(2,1)S(1)}, u32[]{:S(2)}, u32[]{:S(2)}) collective-permute-start(bf16[10,4,4096]{2,1,0:T(4,128)(2,1)} %own_ref.1), channel_id=1, source_target_pairs={{16,32},{32,16},{48,64},{64,48},{80,96},{96,80},{112,128},{128,112... | collective-permute-start | bytes 983048 | tf_op jit(solution)/shard_map/ppermute | solution.py:215
  6.7 10.8 %collective-permute-start.1 = (bf16[10,2,4096]{2,1,0:T(2,128)(2,1)S(1)}, bf16[10,2,4096]{2,1,0:T(2,128)(2,1)S(1)}, u32[]{:S(2)}, u32[]{:S(2)}) collective-permute-start(bf16[10,2,4096]{2,1,0:T(2,128)(2,1)S(1)} %get-tuple-element.15), channel_id=1, source_target_pairs={{32,64},{48,80},{64,32},{80,48},{96,128},{112,144},{128,96},{144,1... | collective-permute-start | bytes 491528 | tf_op jit(solution)/shard_map/ppermute | solution.py:215
  7.3 10.2 %collective-permute-start = (bf16[10,2,4096]{2,1,0:T(2,128)(2,1)S(1)}, bf16[10,2,4096]{2,1,0:T(2,128)(2,1)S(1)}, u32[]{:S(2)}, u32[]{:S(2)}) collective-permute-start(bf16[10,2,4096]{2,1,0:T(2,128)(2,1)S(1)} %get-tuple-element.16), channel_id=1, source_target_pairs={{0,32},{16,48},{32,0},{48,16},{64,96},{80,112},{96,64},{112,80},{1... | collective-permute-start | bytes 491528 | tf_op jit(solution)/shard_map/ppermute | solution.py:215
  14.0 1.0 %copy-start = (bf16[10,4,4096]{2,1,0:T(4,128)(2,1)S(1)}, bf16[10,4,4096]{2,1,0:T(4,128)(2,1)}, u32[]{:S(2)}) copy-start(bf16[10,4,4096]{2,1,0:T(4,128)(2,1)} %own_ref.1) | copy-start | bytes 983044

commit v5 on v4

--- a/solution.py
+++ b/solution.py
@@ -40,9 +40,18 @@
 
 
 def prep_kernel(date_ref, tile_ref, table_ref, lift_ref, depth_ref, point_ref, mean_ref, var_ref,
-                gain_ref, shift_ref, owner_ref, parcel_ref, w0_ref, w1_ref, columns_ref,
-                counts_ref, ids_ref, *, dates):
+                gain_ref, shift_ref, owner_hbm, parcel_hbm, imagery_hbm, w0_ref, w1_ref,
+                columns_ref, counts_ref, ids_ref, own_ref,
+                owner_ref, parcel_ref, arrived, *, dates):
     f32, bf16 = jnp.float32, jnp.bfloat16
+    copies = [
+        pltpu.make_async_copy(source, target, arrived.at[n])
+        for n, (source, target) in enumerate(
+            ((imagery_hbm, own_ref), (owner_hbm, owner_ref), (parcel_hbm, parcel_ref))
+        )
+    ]
+    for copy in copies:
+        copy.start()
     taps = depth_ref.shape[0]
     date_index, tile_index = date_ref[0], tile_ref[0]
     factor = gain_ref[...] / jnp.sqrt(var_ref[...] + EPSILON)
@@ -78,6 +87,9 @@
             depth_ref[k, 1:2, :], (128, 128)
         ).T
     columns_ref[taps * 128 : (taps + 1) * 128, :] = jnp.broadcast_to(shift[1:2], (128, 128)).T
+    copies[0].wait()
+    copies[1].wait()
+    copies[2].wait()
     held = ids_ref.shape[0]
     own = pl.ds(pl.multiple_of(tile_index * held, held), held)
     ids_ref[...] = owner_ref[own, :] * PARC_DEV + parcel_ref[own, :]
@@ -227,7 +239,7 @@
     table = jnp.asarray(column_table(bands, taps))
     vmem = pl.BlockSpec(memory_space=pltpu.VMEM)
     smem = pl.BlockSpec(memory_space=pltpu.SMEM)
-    w0, w1, columns, counts, ids = pl.pallas_call(
+    w0, w1, columns, counts, ids, own = pl.pallas_call(
         functools.partial(prep_kernel, dates=dates),
         out_shape=(
             pltpu.VMEM((12 * channels, 4 * SECTION), jnp.bfloat16),
@@ -235,14 +247,20 @@
             pltpu.VMEM(((taps + 1) * channels, channels), jnp.float32),
             pltpu.VMEM((PARC_DEV, channels), jnp.float32),
             pltpu.VMEM((pix_dev // 128, 128), jnp.int32),
+            pltpu.VMEM(imagery.shape, imagery.dtype),
         ),
-        in_specs=[smem] * 2 + [vmem] * 10,
-        out_specs=(vmem,) * 5,
+        in_specs=[smem] * 2 + [vmem] * 8 + [pl.BlockSpec(memory_space=pltpu.HBM)] * 3,
+        out_specs=(vmem,) * 6,
+        scratch_shapes=[
+            pltpu.VMEM((tiles * pix_dev // 128, 128), jnp.int32),
+            pltpu.VMEM((tiles * pix_dev // 128, 128), jnp.int32),
+            pltpu.SemaphoreType.DMA((3,)),
+        ],
         compiler_params=pltpu.CompilerParams(vmem_limit_bytes=VMEM_LIMIT),
         name="prep",
     )(date_index.reshape(1), tile_index.reshape(1), *far(
         table, lift_weight, depth_weight.transpose(1, 0, 2), point_weight, bn_mean, bn_var,
-        bn_gain, bn_shift, owner.reshape(-1, 128), parcel_local.reshape(-1, 128)))
+        bn_gain, bn_shift, owner.reshape(-1, 128), parcel_local.reshape(-1, 128), imagery))
 
     def near(*arrays):
         return [pltpu.with_memory_space_constraint(x, pltpu.VMEM) for x in arrays]
@@ -255,7 +273,7 @@
         scratch_shapes=[pltpu.VMEM((3 * SECTION, BLOCK), jnp.bfloat16)],
         compiler_params=pltpu.CompilerParams(vmem_limit_bytes=VMEM_LIMIT),
         name="middle",
-    )(date_index.reshape(1), *near(by_partner, imagery, by_across, w0))
+    )(date_index.reshape(1), *near(by_partner, own, by_across, w0))
     sums = pl.pallas_call(
         functools.partial(main_kernel, taps=taps),
         out_shape=jax.ShapeDtypeStruct((tiles * PARC_DEV, channels), jnp.float32),

time: 37.2 us -> 37 us (level)
  local copies, waits for them, and re-layouts: 0.97 us -> 0 us
  Pallas kernels: 9.59 us -> 10.3 us
    unnamed x2 -> x0, local copies, waits for them, and re-layouts: 0.97 us -> none
    pallas_call x1, Pallas kernels: 2.29 us -> 2.9 us  [local(): pl.pallas_call(functools.partial(prep_kernel, dates=dates), out_shape=(pl...]
  transfers between devices with their start and end apart: 4 -> 4, of which waited for: 0 -> 0; matrix products, arithmetic and copies ran while one was open for 4% -> 4% of each run, Pallas kernels for 13% -> 15%
where the time goes in v5:
time: 37 us; the launch traced here: 36.8 us
  blocking collectives  14 us (38%)
  Pallas kernels  10.3 us (28%)
  starting transfers between devices  10.2 us (28%)
  other arithmetic  2.1 us (6%)
    all_to_all x1, blocking collectives, local(): lax.all_to_all(sums, 'tile', split_axis=0, concat_axis=0, tiled=True)  14 us
    ppermute x4, starting transfers between devices, swapped(): lax.ppermute(value, 'date', [(d, t) for d, t in pairs if 0 <= t < dates])  10.2 us
    pallas_call x1, Pallas kernels, local(): pl.pallas_call(functools.partial(main_kernel, taps=taps), out_shape=jax.S...  4.91 us
    pallas_call x1, Pallas kernels, local(): pl.pallas_call(functools.partial(prep_kernel, dates=dates), out_shape=(pl...  2.9 us
    pallas_call x1, Pallas kernels, local(): pl.pallas_call(middle_kernel, out_shape=pltpu.VMEM((4 * channels, pix_dev...  2.49 us
    select_n x1, other arithmetic, local(): by_odd = swapped(jnp.where(chip_odd, last, first), odd_pairs)  1.47 us
  transfers between devices with their start and end apart: 4, of which 0 were waited for; matrix products, arithmetic and copies ran while one was open for 4% of the time, Pallas kernels for 15%

profile of v5, /device:TPU:1, one launch (start us, length us, event | category | flops | bytes accessed | tf_op | source)
XLA Modules:
  0.0 36.8 jit_solution(10422500372681697610)
XLA Ops:
  0.0 3.2 %collective-permute-start.2 = (bf16[10,4,4096]{2,1,0:T(4,128)(2,1)}, bf16[10,4,4096]{2,1,0:T(4,128)(2,1)S(1)}, u32[]{:S(2)}, u32[]{:S(2)}) collective-permute-start(bf16[10,4,4096]{2,1,0:T(4,128)(2,1)} %imagery_hbm.1), channel_id=1, source_target_pairs={{0,16},{16,0},{32,48},{48,32},{64,80},{80,64},{96,112},{112,96},{1... | collective-permute-start | bytes 983048 | tf_op jit(solution)/shard_map/ppermute | solution.py:227
  3.2 1.9 %collective-permute-start.3 = (bf16[10,4,4096]{2,1,0:T(4,128)(2,1)}, bf16[10,4,4096]{2,1,0:T(4,128)(2,1)S(1)}, u32[]{:S(2)}, u32[]{:S(2)}) collective-permute-start(bf16[10,4,4096]{2,1,0:T(4,128)(2,1)} %imagery_hbm.1), channel_id=1, source_target_pairs={{16,32},{32,16},{48,64},{64,48},{80,96},{96,80},{112,128},{128,112... | collective-permute-start | bytes 983048 | tf_op jit(solution)/shard_map/ppermute | solution.py:227
  5.2 1.5 %broadcast_select_fusion = (bf16[10,2,4096]{2,1,0:T(2,128)(2,1)S(1)}, bf16[10,2,4096]{2,1,0:T(2,128)(2,1)S(1)}) fusion(pred[]{:T(512)S(6)} %eq.5, bf16[10,4,4096]{2,1,0:T(4,128)(2,1)} %imagery_hbm.1), kind=kLoop, calls=%fused_computation | loop fusion | flops 163840 | bytes 655361 | tf_op jit(solution)/shard_map/jit(_where)/select_n | solution.py:234
  6.7 0.7 %collective-permute-start.1 = (bf16[10,2,4096]{2,1,0:T(2,128)(2,1)S(1)}, bf16[10,2,4096]{2,1,0:T(2,128)(2,1)S(1)}, u32[]{:S(2)}, u32[]{:S(2)}) collective-permute-start(bf16[10,2,4096]{2,1,0:T(2,128)(2,1)S(1)} %get-tuple-element.17), channel_id=1, source_target_pairs={{32,64},{48,80},{64,32},{80,48},{96,128},{112,144},{128,96},{144,1... | collective-permute-start | bytes 491528 | tf_op jit(solution)/shard_map/ppermute | solution.py:227
  7.3 4.4 %collective-permute-start = (bf16[10,2,4096]{2,1,0:T(2,128)(2,1)S(1)}, bf16[10,2,4096]{2,1,0:T(2,128)(2,1)S(1)}, u32[]{:S(2)}, u32[]{:S(2)}) collective-permute-start(bf16[10,2,4096]{2,1,0:T(2,128)(2,1)S(1)} %get-tuple-element.18), channel_id=1, source_target_pairs={{0,32},{16,48},{32,0},{48,16},{64,96},{80,112},{96,64},{112,80},{1... | collective-permute-start | bytes 491528 | tf_op jit(solution)/shard_map/ppermute | solution.py:227
  11.7 2.9 %prep.1 = (bf16[1536,192]{1,0:T(8,128)(2,1)S(1)}, bf16[128,256]{1,0:T(8,128)(2,1)S(1)}, f32[768,128]{1,0:T(8,128)S(1)}, f32[16,128]{1,0:T(8,128)S(1)}, s32[32,12...) custom-call(s32[1]{0:T(128)} %bitcast.date_ref, s32[1]{0:T(128)} %bitcast.1.tile_ref, s32[12,192]{1,0:T(8,128)} %constant.38.clone.table_ref, ...), custom_call_target="tpu_custom_call" | custom-call | tf_op jit(solution)/shard_map/prep/pallas_call | solution.py:242
  14.6 0.0 collective-permute-done.2.partner_ref
  14.6 0.0 collective-permute-done.3.across_ref
  14.7 2.5 %middle.1.middle_ref = bf16[512,4096]{1,0:T(8,128)(2,1)S(1)} custom-call(s32[1]{0:T(128)} %bitcast.date_ref, bf16[10,4,4096]{2,1,0:T(4,128)(2,1)S(1)} %collective-permute-done.2.partner_ref, bf16[10,4,4096]{2,1,0:T(4,128)(2,1)S(1)} %get-tuple-element.15.own_ref, bf16[10,4,4096]{2,1,0:T(4,128)(2,1)S(1)} %collective-permute-done.3.across_ref, ...), custom_call_target="tpu_custom_call" | custom-call | tf_op jit(solution)/shard_map/middle/pallas_call | solution.py:268
  17.1 0.0 collective-permute-done.1.odd_ref
  17.2 0.0 collective-permute-done.even_ref
  17.2 4.9 %encode.1 = f32[256,128]{1,0:T(8,128)S(1)} custom-call(s32[1]{0:T(128)} %bitcast.date_ref, bf16[10,2,4096]{2,1,0:T(2,128)(2,1)S(1)} %collective-permute-done.even_ref, bf16[10,2,4096]{2,1,0:T(2,128)(2,1)S(1)} %collective-permute-done.1.odd_ref, bf16[10,4,4096]{2,1,0:T(4,128)(2,1)S(1)} %collective-permute-done.2.partner_ref, ...), custom_call_target="tpu_custom_call" | custom-call | tf_op jit(solution)/shard_map/encode/pallas_call | solution.py:277
  22.1 14.0 %all_to_all.9 = f32[16,16,128]{2,1,0:T(8,128)S(1)} all-to-all(f32[16,16,128]{2,1,0:T(8,128)S(1)} %bitcast.8), channel_id=1, replica_groups=mesh['date'=16,'tile'=16] {'tile'}, dimensions={0} | all-to-all | bytes 262144 | tf_op jit(solution)/shard_map/all_to_all | solution.py:287
  36.1 0.6 %divide_bitcast_fusion = f32[1,16,128]{2,1,0:T(8,128)} fusion(f32[16,128]{1,0:T(8,128)S(1)} %reduce_sum.9, f32[16,128]{1,0:T(8,128)S(1)} %get-tuple-element.16), kind=kLoop, calls=%fused_computation.2 | loop fusion | flops 4096 | bytes 24576 | tf_op jit(solution)/shard_map/broadcast_in_dim | solution.py:289
  (1 shorter events, 0.0 us)
Async XLA Ops:
  0.0 14.6 %collective-permute-start.2 = (bf16[10,4,4096]{2,1,0:T(4,128)(2,1)}, bf16[10,4,4096]{2,1,0:T(4,128)(2,1)S(1)}, u32[]{:S(2)}, u32[]{:S(2)}) collective-permute-start(bf16[10,4,4096]{2,1,0:T(4,128)(2,1)} %imagery_hbm.1), channel_id=1, source_target_pairs={{0,16},{16,0},{32,48},{48,32},{64,80},{80,64},{96,112},{112,96},{1... | collective-permute-start | bytes 983048 | tf_op jit(solution)/shard_map/ppermute | solution.py:227
  3.2 11.4 %collective-permute-start.3 = (bf16[10,4,4096]{2,1,0:T(4,128)(2,1)}, bf16[10,4,4096]{2,1,0:T(4,128)(2,1)S(1)}, u32[]{:S(2)}, u32[]{:S(2)}) collective-permute-start(bf16[10,4,4096]{2,1,0:T(4,128)(2,1)} %imagery_hbm.1), channel_id=1, source_target_pairs={{16,32},{32,16},{48,64},{64,48},{80,96},{96,80},{112,128},{128,112... | collective-permute-start | bytes 983048 | tf_op jit(solution)/shard_map/ppermute | solution.py:227
  6.7 10.5 %collective-permute-start.1 = (bf16[10,2,4096]{2,1,0:T(2,128)(2,1)S(1)}, bf16[10,2,4096]{2,1,0:T(2,128)(2,1)S(1)}, u32[]{:S(2)}, u32[]{:S(2)}) collective-permute-start(bf16[10,2,4096]{2,1,0:T(2,128)(2,1)S(1)} %get-tuple-element.17), channel_id=1, source_target_pairs={{32,64},{48,80},{64,32},{80,48},{96,128},{112,144},{128,96},{144,1... | collective-permute-start | bytes 491528 | tf_op jit(solution)/shard_map/ppermute | solution.py:227
  7.3 9.8 %collective-permute-start = (bf16[10,2,4096]{2,1,0:T(2,128)(2,1)S(1)}, bf16[10,2,4096]{2,1,0:T(2,128)(2,1)S(1)}, u32[]{:S(2)}, u32[]{:S(2)}) collective-permute-start(bf16[10,2,4096]{2,1,0:T(2,128)(2,1)S(1)} %get-tuple-element.18), channel_id=1, source_target_pairs={{0,32},{16,48},{32,0},{48,16},{64,96},{80,112},{96,64},{112,80},{1... | collective-permute-start | bytes 491528 | tf_op jit(solution)/shard_map/ppermute | solution.py:227
